TPU v7x, 32 devices: a whole 2x2x4 slice. The times are simulated.
32 devices in a mesh: ray: 4 (over x, core), vox: 8 (over z, y).
Axes of the slice: x: 2, y: 2, z: 4, core: 2. Of those that a mesh axis runs over, the one named last changes fastest.
Arguments:
- tiles: float32 [2048, 128, 128], P(('ray', 'vox')), may hold values from -0.25 to 0.25
- tile_ray: int32 [2048], P(('ray', 'vox')), may hold values from 0 to 15
- tile_vox: int32 [2048], P(('ray', 'vox')), may hold values from 0 to 511, as said below
- tile_count: int32 [32], P(('ray', 'vox')), may hold values from 1 to 64, as said below
- travel: float32 [512, 128], P(('ray', 'vox')), may hold values from -6 to 6
Outputs:
- solution: float32 [512, 128], P('vox')
- direction: float32 [512, 128], P('vox')
Inputs may be any that keep to these rules, and one draw needn't show every extreme that they name: `tile_count`: each entry is 1 to 64; some device has exactly 64 live slots. Among the 64 slots of one device (live or not), at most 16 have voxel blocks in the same range of 64 blocks (same tile_vox // 64); on every device some range is named by exactly 16 slots.
All inputs are finite; a program needn't handle non-finite values.
Results may differ from a plain program's by a relative error of at most 0.00017.
Values sent between devices are 32-bit elements; how exact they have to be, the bound alone decides.
No kernel may reach another device: no remote copies, remote signals or barrier semaphores. Data moves between devices by JAX's collectives and lax.ppermute only.
A program may use at most 64 MiB of HBM per device.

v0:
```python
import jax
import jax.numpy as jnp
from jax import lax
from jax.sharding import PartitionSpec as P

VBD = 64
ITERS = 2


HIGH = lax.Precision.HIGHEST


def on_device(tiles, tile_ray, tile_vox, tile_count, travel):
    n_vox = lax.axis_size("vox")
    blocks_all = VBD * n_vox
    tile_num = tiles.shape[0]
    ray_blocks = travel.shape[0]
    width = travel.shape[1]
    live = (jnp.arange(tile_num, dtype=jnp.int32) < tile_count[0]).astype(jnp.float32)[:, None]
    selector = (tile_ray[None, :] == jnp.arange(ray_blocks, dtype=jnp.int32)[:, None]).astype(
        jnp.float32
    )

    def backward(ray_vec):
        rows_in = jnp.dot(selector.T, ray_vec, precision=HIGH)
        prod = jnp.einsum("tij,ti->tj", tiles, rows_in, precision=HIGH) * live
        partial_sum = jnp.zeros((blocks_all, width), jnp.float32).at[tile_vox].add(prod)
        owned = lax.psum_scatter(partial_sum, "vox", scatter_dimension=0, tiled=True)
        return lax.psum(owned, "ray")

    def ray_length(ray_vec):
        return jnp.sqrt(lax.psum(jnp.sum(ray_vec * ray_vec), ("ray", "vox")))

    def vox_length(vox_vec):
        return jnp.sqrt(lax.psum(jnp.sum(vox_vec * vox_vec), "vox"))

    beta_now = ray_length(travel)
    ray_vec = travel / beta_now
    vox_vec = backward(ray_vec)
    alpha_now = vox_length(vox_vec)
    vox_vec = vox_vec / alpha_now
    direction = vox_vec
    solution = jnp.zeros_like(vox_vec)
    phibar = beta_now
    rhobar = alpha_now
    for step in range(ITERS):
        whole = lax.all_gather(vox_vec, "vox", axis=0, tiled=True)
        forward_prod = jnp.einsum("tij,tj->ti", tiles, whole[tile_vox], precision=HIGH) * live
        ray_vec = jnp.dot(selector, forward_prod, precision=HIGH) - alpha_now * ray_vec
        beta_now = ray_length(ray_vec)
        ray_vec = ray_vec / beta_now
        vox_vec = backward(ray_vec) - beta_now * vox_vec
        alpha_now = vox_length(vox_vec)
        vox_vec = vox_vec / alpha_now
        rho_val = jnp.sqrt(rhobar * rhobar + beta_now * beta_now)
        cosine = rhobar / rho_val
        sine_val = beta_now / rho_val
        theta_val = sine_val * alpha_now
        rhobar = -cosine * alpha_now
        phi_val = cosine * phibar
        phibar = sine_val * phibar
        solution = solution + phi_val / rho_val * direction
        direction = vox_vec - theta_val / rho_val * direction
    return (solution, direction)


def solution(mesh):
    return jax.shard_map(
        on_device,
        mesh=mesh,
        in_specs=(
            P(("ray", "vox"), None, None),
            P(("ray", "vox")),
            P(("ray", "vox")),
            P(("ray", "vox")),
            P(("ray", "vox"), None),
        ),
        out_specs=(P("vox", None), P("vox", None)),
        check_vma=False,
    )
```

profile of v0, /device:TPU:0, one launch (start us, length us, event | category | flops | bytes accessed | tf_op | source)
XLA Modules:
  0.0 524.2 jit_solution(6376675607895804721)
XLA Ops:
  7.2 1.3 multiply_reduce_fusion.5
  8.5 42.2 %psum.63 = f32[]{:T(128)} all-reduce(f32[]{:T(128)} %multiply_reduce_fusion.5), channel_id=1, replica_groups=mesh['ray'=4,'vox'=8] {'ray','vox'}, use_global_device_ids=true, to_apply=%region_1.0 | all-reduce | flops 1 | bytes 8 | tf_op jit(solution)/shard_map/psum | solution.py:32
  52.7 0.9 fusion.19
  53.7 5.3 %fusion.26 = f32[64,1,128]{2,1,0:T(1,128)S(1)} fusion(f32[64,128,1]{1,2,0:T(1,128)S(1)} %bitcast.43, f32[64,128,128]{2,1,0:T(8,128)} %param.5), kind=kOutput, calls=%fused_computation.52 | convolution fusion | flops 12582912 | bytes 4259840 | tf_op jit(solution)/shard_map/tij,ti->tj/dot_general | solution.py:26
  59.0 1.5 scatter_custom_fusion
  60.6 61.7 %reduce-scatter.4.cloned.1.call-done = f32[64,128]{1,0:T(8,128)} async-done(((f32[512,128]{1,0:T(8,128)}), f32[64,128]{1,0:T(8,128)}) %reduce-scatter.4.cloned.1.call-update) | async-done | bytes 32784 | tf_op jit(solution)/shard_map/reduce_scatter | solution.py:28
  122.3 10.8 %psum.64 = f32[64,128]{1,0:T(8,128)S(1)} all-reduce(f32[64,128]{1,0:T(8,128)} %reduce-scatter.4.cloned.1.call-done), channel_id=1, replica_groups=mesh['ray'=4,'vox'=8] {'ray'}, use_global_device_ids=true, to_apply=%region_4.0 | all-reduce | flops 8192 | bytes 65536 | tf_op jit(solution)/shard_map/psum | solution.py:29
  133.7 20.1 %psum.65 = f32[]{:T(128)} all-reduce(f32[]{:T(128)} %multiply_reduce_fusion.2), channel_id=1, replica_groups=mesh['ray'=4,'vox'=8] {'vox'}, use_global_device_ids=true, to_apply=%region_6.0 | all-reduce | flops 1 | bytes 8 | tf_op jit(solution)/shard_map/psum | solution.py:35
  154.5 30.9 %all_gather.6 = f32[512,128]{1,0:T(8,128)S(1)} all-gather(f32[64,128]{1,0:T(8,128)S(1)} %broadcast_divide_fusion.1), channel_id=1, replica_groups=mesh['ray'=4,'vox'=8] {'vox'}, dimensions={0}, use_global_device_ids=true | all-gather | bytes 294912 | tf_op jit(solution)/shard_map/all_gather | solution.py:47
  186.0 8.3 %fusion.27 = f32[64,1,128]{2,1,0:T(1,128)S(1)} fusion(f32[64,128,1]{1,2,0:T(1,128)S(1)} %bitcast.40, f32[64,128,128]{2,1,0:T(8,128)} %param.5), kind=kOutput, calls=%fused_computation.53 | convolution fusion | flops 12582912 | bytes 4259840 | tf_op jit(solution)/shard_map/tij,tj->ti/dot_general | solution.py:48
  195.2 37.1 %psum.66 = f32[]{:T(128)} all-reduce(f32[]{:T(128)} %get-tuple-element.4), channel_id=1, replica_groups=mesh['ray'=4,'vox'=8] {'ray','vox'}, use_global_device_ids=true, to_apply=%region_8.0 | all-reduce | flops 1 | bytes 8 | tf_op jit(solution)/shard_map/psum | solution.py:32
  233.2 5.3 %fusion.28 = f32[64,1,128]{2,1,0:T(1,128)S(1)} fusion(f32[64,128,1]{1,2,0:T(1,128)S(1)} %bitcast.44, f32[64,128,128]{2,1,0:T(8,128)} %param.5), kind=kOutput, calls=%fused_computation.54 | convolution fusion | flops 12582912 | bytes 4259840 | tf_op jit(solution)/shard_map/tij,ti->tj/dot_general | solution.py:26
  238.5 1.5 scatter_custom_fusion.1
  240.1 63.4 %reduce-scatter.6.cloned.1.call-done = f32[64,128]{1,0:T(8,128)} async-done(((f32[512,128]{1,0:T(8,128)}), f32[64,128]{1,0:T(8,128)}) %reduce-scatter.6.cloned.1.call-update) | async-done | bytes 32784 | tf_op jit(solution)/shard_map/reduce_scatter | solution.py:28
  303.4 10.8 %psum.67 = f32[64,128]{1,0:T(8,128)S(1)} all-reduce(f32[64,128]{1,0:T(8,128)} %reduce-scatter.6.cloned.1.call-done), channel_id=1, replica_groups=mesh['ray'=4,'vox'=8] {'ray'}, use_global_device_ids=true, to_apply=%region_11.0 | all-reduce | flops 8192 | bytes 65536 | tf_op jit(solution)/shard_map/psum | solution.py:29
  314.9 20.1 %psum.68 = f32[]{:T(128)} all-reduce(f32[]{:T(128)} %multiply_reduce_fusion.1), channel_id=1, replica_groups=mesh['ray'=4,'vox'=8] {'vox'}, use_global_device_ids=true, to_apply=%region_13.0 | all-reduce | flops 1 | bytes 8 | tf_op jit(solution)/shard_map/psum | solution.py:35
  335.7 31.1 %all_gather.7 = f32[512,128]{1,0:T(8,128)S(1)} all-gather(f32[64,128]{1,0:T(8,128)S(1)} %broadcast_divide_fusion), channel_id=1, replica_groups=mesh['ray'=4,'vox'=8] {'vox'}, dimensions={0}, use_global_device_ids=true | all-gather | bytes 294912 | tf_op jit(solution)/shard_map/all_gather | solution.py:47
  367.3 8.3 %fusion.29 = f32[64,1,128]{2,1,0:T(1,128)S(1)} fusion(f32[64,128,1]{1,2,0:T(1,128)S(1)} %bitcast.38, f32[64,128,128]{2,1,0:T(8,128)} %param.5), kind=kOutput, calls=%fused_computation.55 | convolution fusion | flops 12582912 | bytes 4259840 | tf_op jit(solution)/shard_map/tij,tj->ti/dot_general | solution.py:48
  376.5 37.1 %psum.69 = f32[]{:T(128)} all-reduce(f32[]{:T(128)} %get-tuple-element.6), channel_id=1, replica_groups=mesh['ray'=4,'vox'=8] {'ray','vox'}, use_global_device_ids=true, to_apply=%region_15.0 | all-reduce | flops 1 | bytes 8 | tf_op jit(solution)/shard_map/psum | solution.py:32
  414.5 5.3 %fusion.30 = f32[64,1,128]{2,1,0:T(1,128)S(1)} fusion(f32[64,128,1]{1,2,0:T(1,128)S(1)} %bitcast.42, f32[64,128,128]{2,1,0:T(8,128)} %param.5), kind=kOutput, calls=%fused_computation.56 | convolution fusion | flops 12582912 | bytes 4259840 | tf_op jit(solution)/shard_map/tij,ti->tj/dot_general | solution.py:26
  419.8 1.5 scatter_custom_fusion.2
  421.7 63.1 %reduce-scatter.8.cloned.1.call-done = f32[64,128]{1,0:T(8,128)} async-done(((f32[512,128]{1,0:T(8,128)}), f32[64,128]{1,0:T(8,128)}) %reduce-scatter.8.cloned.1.call-update) | async-done | bytes 32784 | tf_op jit(solution)/shard_map/reduce_scatter | solution.py:28
  484.8 10.8 %psum.70 = f32[64,128]{1,0:T(8,128)S(1)} all-reduce(f32[64,128]{1,0:T(8,128)} %reduce-scatter.8.cloned.1.call-done), channel_id=1, replica_groups=mesh['ray'=4,'vox'=8] {'ray'}, use_global_device_ids=true, to_apply=%region_18.0 | all-reduce | flops 8192 | bytes 65536 | tf_op jit(solution)/shard_map/psum | solution.py:29
  496.3 20.0 %psum.71 = f32[]{:T(128)} all-reduce(f32[]{:T(128)} %multiply_reduce_fusion), channel_id=1, replica_groups=mesh['ray'=4,'vox'=8] {'vox'}, use_global_device_ids=true, to_apply=%region_20.0 | all-reduce | flops 1 | bytes 8 | tf_op jit(solution)/shard_map/psum | solution.py:35
  (25 shorter events, 6.6 us)
Async XLA Ops:
  7.2 115.2 %reduce-scatter.4.cloned.1.call-start = ((), (), s32[]{:S(2)}) async-start(), calls=%async_computation.3 | async-start | bytes 294912 | tf_op jit(solution)/shard_map/reduce_scatter | solution.py:28
  53.7 140.7 %copy-start = (f32[16,128]{1,0:T(8,128)S(1)}, f32[16,128]{1,0:T(8,128)}, u32[]{:S(2)}) copy-start(f32[16,128]{1,0:T(8,128)} %param.9) | copy-start | bytes 24580
  53.7 140.7 %copy-start.1 = (s32[64]{0:T(128)S(1)}, s32[64]{0:T(128)}, u32[]{:S(2)}) copy-start(s32[64]{0:T(128)} %param.6) | copy-start | bytes 772
  60.5 242.9 %reduce-scatter.6.cloned.1.call-start = ((), (), s32[]{:S(2)}) async-start(), calls=%async_computation.4 | async-start | bytes 294912 | tf_op jit(solution)/shard_map/reduce_scatter | solution.py:28
  240.0 244.8 %reduce-scatter.8.cloned.1.call-start = ((), (), s32[]{:S(2)}) async-start(), calls=%async_computation.5 | async-start | bytes 294912 | tf_op jit(solution)/shard_map/reduce_scatter | solution.py:28
Sparse Core Ops, SparseCore 0:
  60.7 61.6 reduce-scatter.3
  240.2 63.2 reduce-scatter.5
  421.5 63.2 reduce-scatter.7
where the time goes:
time: 526 us; the launch traced here: 524 us
  blocking collectives  271 us (52%)
  waiting for transfers between devices  188 us (36%)
  matrix products  35.5 us (7%)
  between operations  19.1 us (4%)
  other arithmetic  9.11 us (2%)
    reduce_scatter x3, waiting for transfers between devices, backward(): lax.psum_scatter(partial_sum, 'vox', scatter_dimension=0, tiled=True)  188 us
    psum x3, blocking collectives, ray_length(): return jnp.sqrt(lax.psum(jnp.sum(ray_vec * ray_vec), ('ray', 'vox')))  116 us
    all_gather x2, blocking collectives, on_device(): whole = lax.all_gather(vox_vec, 'vox', axis=0, tiled=True)  62 us
    psum x3, blocking collectives, vox_length(): return jnp.sqrt(lax.psum(jnp.sum(vox_vec * vox_vec), 'vox'))  60.2 us
    psum x3, blocking collectives, backward(): return lax.psum(owned, 'ray')  32.4 us
    dot_general x2, matrix products, on_device(): jnp.einsum('tij,tj->ti', tiles, whole[tile_vox], precision=HIGH) * live  16.6 us
    dot_general x3, matrix products, backward(): prod = jnp.einsum('tij,ti->tj', tiles, rows_in, precision=HIGH) * live  15.8 us
  transfers between devices with their start and end apart: 3, of which 3 were waited for; matrix products, arithmetic and copies ran while one was open for 0% of the time, Pallas kernels for 0%

commit v1 on v0

v1 whole, which is shorter than its diff:
```python
import functools

import jax
import jax.numpy as jnp
from jax import lax
from jax.experimental import pallas as pl
from jax.experimental.pallas import tpu as pltpu
from jax.sharding import PartitionSpec as P

VBD = 64
LANES = 128
GROUP = 8
F32 = jnp.float32
BF16 = jnp.bfloat16


class Sizes:
    def __init__(self, n_ray, n_vox, slots, ray_blocks):
        self.n_ray, self.n_vox, self.slots, self.ray_blocks = n_ray, n_vox, slots, ray_blocks
        self.peers = n_ray * n_vox
        self.cap = 2 * slots // n_vox
        self.seg = LANES // n_ray
        self.data_rows = max(1, self.cap * self.seg // LANES)
        self.segs = self.cap // self.data_rows
        self.rows = self.data_rows + 1
        self.compact = self.cap * n_vox


def lane(shape):
    return lax.broadcasted_iota(jnp.int32, shape, len(shape) - 1)


def total(x):
    return jnp.sum(jnp.sum(x, axis=1, keepdims=True), axis=0, keepdims=True)


def pick(row, k):
    return jnp.sum(jnp.where(lane(row.shape) == k, row, 0.0), axis=1, keepdims=True)


def shift_lanes(x, amount):
    amount = amount % LANES
    return x if amount == 0 else pltpu.roll(x, amount, axis=1)


def split3(x):
    hi = x.astype(BF16)
    rest = x - hi.astype(F32)
    mid = rest.astype(BF16)
    low = (rest - mid.astype(F32)).astype(BF16)
    return jnp.concatenate([hi, mid, low], axis=1)


def select_dot(onehot, x):
    width = x.shape[1]
    out = jnp.dot(onehot, split3(x), preferred_element_type=F32)
    return out[:, :width] + out[:, width : 2 * width] + out[:, 2 * width :]


def tile_copies(tiles_hbm, tiles_v, sem, slots):
    return [
        pltpu.make_async_copy(
            tiles_hbm.at[pl.ds(c * GROUP, GROUP)], tiles_v.at[pl.ds(c * GROUP, GROUP)], sem.at[c]
        )
        for c in range(slots // GROUP)
    ]


def wait_group(tiles_hbm, tiles_v, sem, c):
    pltpu.make_async_copy(
        tiles_hbm.at[pl.ds(c * GROUP, GROUP)], tiles_v.at[pl.ds(c * GROUP, GROUP)], sem.at[c]
    ).wait()


def write_products(z, prod, msg, meta):
    segment = lane((z.n_vox, LANES)) // z.seg
    for q in range(z.data_rows):
        part = [
            prod[pl.ds((q * z.segs + g) * z.n_vox, z.n_vox), :] for g in range(z.segs)
        ]
        for r in range(z.n_ray):
            out = jnp.zeros((z.n_vox, LANES), F32)
            for g in range(z.segs):
                out = jnp.where(segment == g, shift_lanes(part[g], (g - r) * z.seg), out)
            msg[pl.ds(r * z.n_vox * z.rows + q, z.n_vox, stride=z.rows), :] = out
    for r in range(z.n_ray):
        msg[pl.ds(r * z.n_vox * z.rows + z.data_rows, z.n_vox, stride=z.rows), :] = jnp.where(
            lane((z.n_vox, LANES)) == z.cap + 1, jnp.float32(r), meta
        )


def backward(z, where_of, tiles_v, rays_wide, prod, wait):
    def step(c, carry):
        if wait is not None:
            wait(c)
        for s in range(GROUP):
            t = c * GROUP + s
            ray, row = where_of(t)
            block = rays_wide[pl.ds(ray * LANES, LANES), :]
            prod[pl.ds(row, 1), :] = jnp.sum(tiles_v[t] * block, axis=0, keepdims=True)
        return carry

    lax.fori_loop(0, z.slots // GROUP, step, 0)


def first_kernel(
    z, tile_ray, tile_vox, tile_count, travel, tiles_hbm, msg, cols, code,
    tiles_v, rays_wide, prod, named, pad, count, sem,
):
    for copy in tile_copies(tiles_hbm, tiles_v, sem, z.slots):
        copy.start()
    for o in range(z.n_vox):
        count[o] = 0
    prod[...] = jnp.zeros_like(prod)
    named[...] = jnp.full_like(named, -1.0)
    pad[...] = jnp.zeros_like(pad)
    pad[pl.ds(0, z.ray_blocks), :] = travel[...]
    by_col = pad[...].T
    cols[...] = by_col
    for r in range(z.ray_blocks):
        rays_wide[pl.ds(r * LANES, LANES), :] = jnp.broadcast_to(
            by_col[:, r : r + 1], (LANES, LANES)
        )
    live = tile_count[0]

    def where_of(t):
        vox, ray = tile_vox[t], tile_ray[t]
        owner = vox // VBD
        k = count[owner]
        count[owner] = k + 1
        row = k * z.n_vox + owner
        code[t] = row * 256 + ray
        block = jnp.where(t < live, vox - owner * VBD, -1).astype(F32)
        named[pl.ds(row, 1), :] = jnp.full((1, LANES), block, F32)
        return ray, row

    backward(
        z, where_of, tiles_v, rays_wide, prod,
        lambda c: wait_group(tiles_hbm, tiles_v, sem, c),
    )
    here = lane((z.n_vox, LANES))
    meta = jnp.where(here == z.cap, total(travel[...] * travel[...]), 0.0)
    for k in range(z.cap):
        meta = jnp.where(here == k, named[pl.ds(k * z.n_vox, z.n_vox), :], meta)
    write_products(z, prod, msg, meta)


def middle_kernel(
    z, code, back, old_cols, tiles_hbm, msg, cols, scal,
    tiles_v, rays_wide, prod, vox_rows, sums, sems, sem,
):
    for copy in tile_copies(tiles_hbm, tiles_v, sem, z.slots):
        copy.start()
    meta = back[pl.ds(z.data_rows, z.peers, stride=z.rows), :]
    alpha = jnp.sqrt(pick(jnp.sum(meta, axis=0, keepdims=True), 0))
    beta = pick(meta[0:1], 1)
    here = lane((8, LANES))
    scal[...] = jnp.where(here == 0, alpha, jnp.where(here == 1, beta, 0.0))
    segment = lane((z.n_vox, LANES)) // z.seg
    for q in range(z.data_rows):
        part = [
            back[pl.ds(r * z.n_vox * z.rows + q, z.n_vox, stride=z.rows), :]
            for r in range(z.n_ray)
        ]
        for g in range(z.segs):
            row = jnp.zeros((z.n_vox, LANES), F32)
            for r in range(z.n_ray):
                row = jnp.where(segment == r, shift_lanes(part[r], (r - g) * z.seg), row)
            vox_rows[pl.ds((q * z.segs + g) * z.n_vox, z.n_vox), :] = row / alpha
    sums[...] = jnp.zeros_like(sums)
    sems[...] = jnp.zeros_like(sems)
    prod[...] = jnp.zeros_like(prod)

    def where_of(t):
        both = code[t]
        return both & 255, both // 256

    def step(c, carry):
        wait_group(tiles_hbm, tiles_v, sem, c)
        for s in range(GROUP):
            t = c * GROUP + s
            ray, row = where_of(t)
            into = sums if s % 2 == 0 else sems
            into[pl.ds(ray * LANES, LANES), :] += tiles_v[t] * vox_rows[pl.ds(row, 1), :]
        return carry

    lax.fori_loop(0, z.slots // GROUP, step, 0)
    at = lane((LANES, LANES))
    before = old_cols[...] / beta
    now = jnp.zeros((LANES, LANES), F32)
    for r in range(z.ray_blocks):
        both = sums[pl.ds(r * LANES, LANES), :] + sems[pl.ds(r * LANES, LANES), :]
        u = jnp.sum(both, axis=1, keepdims=True) - alpha * before[:, r : r + 1]
        wide = jnp.broadcast_to(u, (LANES, LANES))
        rays_wide[pl.ds(r * LANES, LANES), :] = wide
        now = jnp.where(at == r, wide, now)
    cols[...] = now
    backward(z, where_of, tiles_v, rays_wide, prod, None)
    meta = jnp.where(lane((z.n_vox, LANES)) == z.cap, total(now * now), 0.0)
    write_products(z, prod, msg, meta)


def one_hots(z, meta, onehot, onehot_t):
    wide = jnp.concatenate(
        [shift_lanes(meta, -q * z.segs) for q in range(z.data_rows)], axis=0
    )
    n = z.data_rows * z.peers
    tall = wide.T
    block = lax.broadcasted_iota(jnp.int32, (VBD, n), 0).astype(F32)
    for g in range(z.segs):
        onehot[pl.ds(g * VBD, VBD), :] = (tall[g : g + 1, :] == block).astype(F32).astype(BF16)
    here = lane((n, LANES))
    local = (here % VBD).astype(F32)
    per = LANES // VBD
    for h in range(z.segs // per):
        named = wide[:, h * per : h * per + 1]
        for e in range(1, per):
            named = jnp.where(here // VBD == e, wide[:, h * per + e : h * per + e + 1], named)
        onehot_t[:, pl.ds(h * LANES, LANES)] = (named == local).astype(F32).astype(BF16)


def own_sum(z, msg, onehot):
    data = jnp.concatenate(
        [msg[pl.ds(q, z.peers, stride=z.rows), :] for q in range(z.data_rows)], axis=0
    )
    part = select_dot(onehot[...], data)
    segment = lane((VBD, LANES)) // z.seg
    out = jnp.zeros((VBD, LANES), F32)
    for g in range(z.segs):
        out = jnp.where(segment == g, part[g * VBD : (g + 1) * VBD], out)
    step = LANES // 2
    while step >= z.seg:
        out = out + shift_lanes(out, step)
        step //= 2
    return out


def give_back(z, y, onehot_t, beta, back):
    segment = lane((VBD, LANES)) // z.seg
    square = total(jnp.where(segment == 0, y * y, 0.0))
    spread = jnp.concatenate(
        [jnp.where(segment == g, y, 0.0) for g in range(z.segs)], axis=0
    )
    data = select_dot(onehot_t[...], spread)
    for q in range(z.data_rows):
        back[pl.ds(q, z.peers, stride=z.rows), :] = data[q * z.peers : (q + 1) * z.peers]
    here = lane((z.peers, LANES))
    back[pl.ds(z.data_rows, z.peers, stride=z.rows), :] = jnp.where(
        here == 0, square, jnp.where(here == 1, beta, 0.0)
    )


def message_beta(z, msg):
    meta = msg[pl.ds(z.data_rows, z.peers, stride=z.rows), :]
    return meta, jnp.sqrt(pick(jnp.sum(meta, axis=0, keepdims=True), z.cap))


def owner_first_kernel(z, msg, back, y_out, onehot, onehot_t):
    meta, beta = message_beta(z, msg)
    one_hots(z, meta, onehot, onehot_t)
    y = own_sum(z, msg, onehot) / beta
    y_out[...] = y
    give_back(z, y, onehot_t, beta, back)


def owner_next_kernel(z, msg, onehot, onehot_t, scal, y_in, back, y_out):
    _, beta = message_beta(z, msg)
    alpha = scal[0:1, 0:1]
    y = own_sum(z, msg, onehot) / beta - beta * (y_in[...] / alpha)
    y_out[...] = y
    give_back(z, y, onehot_t, beta, back)


def owner_last_kernel(z, msg, onehot, scal1, scal2, y1, y2, share, back):
    meta, beta3 = message_beta(z, msg)
    mine = pick(meta[0:1], z.cap + 1)
    alpha1, beta1 = scal1[0:1, 0:1], scal1[0:1, 1:2]
    alpha2, beta2 = scal2[0:1, 0:1], scal2[0:1, 1:2]
    v1, v2 = y1[...] / alpha1, y2[...] / alpha2
    w = own_sum(z, msg, onehot) / beta3 - beta3 * v2
    rho1 = jnp.sqrt(alpha1 * alpha1 + beta2 * beta2)
    c1, s1 = alpha1 / rho1, beta2 / rho1
    solution = c1 * beta1 / rho1 * v1
    direction = v2 - s1 * alpha2 / rho1 * v1
    rhobar, phibar = -c1 * alpha2, s1 * beta1
    rho2 = jnp.sqrt(rhobar * rhobar + beta3 * beta3)
    solution = solution + (rhobar / rho2) * phibar / rho2 * direction
    segment = lane((VBD, LANES)) // z.seg
    keep = segment.astype(F32) == mine
    share[pl.ds(0, VBD), :] = jnp.where(keep, w, 0.0)
    share[pl.ds(VBD, VBD), :] = jnp.where(keep, solution, 0.0)
    share[pl.ds(2 * VBD, VBD), :] = jnp.where(keep, direction, 0.0)
    here = lane((z.peers, LANES))
    square = total(jnp.where(segment == 0, w * w, 0.0))
    back[...] = jnp.where(
        here == 0, square, jnp.where(here == 1, beta3 / rho2 / rho2, 0.0)
    )


def final_kernel(z, back, *refs):
    shares, solution, direction = refs[:-2], refs[-2], refs[-1]
    whole = shares[0][...]
    for share in shares[1:]:
        whole = whole + share[...]
    alpha = jnp.sqrt(pick(jnp.sum(back[...], axis=0, keepdims=True), 0))
    factor = pick(back[0:1, :], 1) * alpha
    solution[...] = whole[VBD : 2 * VBD]
    direction[...] = whole[:VBD] / alpha - factor * whole[2 * VBD :]


SMEM = pl.BlockSpec(memory_space=pltpu.SMEM)
VMEM = pl.BlockSpec(memory_space=pltpu.VMEM)
ANY = pl.BlockSpec(memory_space=pl.ANY)
PARAMS = pltpu.CompilerParams(vmem_limit_bytes=24 * 1024 * 1024)


def f32(*shape):
    return jax.ShapeDtypeStruct(shape, F32)


def on_device(tiles, tile_ray, tile_vox, tile_count, travel):
    n_ray, n_vox = lax.axis_size("ray"), lax.axis_size("vox")
    z = Sizes(n_ray, n_vox, tiles.shape[0], travel.shape[0])
    message = f32(z.peers * z.rows, LANES)
    square = f32(LANES, LANES)
    owned = f32(VBD, LANES)

    def call(kernel, name, in_specs, out_shape, out_specs, *args, scratch=()):
        return pl.pallas_call(
            functools.partial(kernel, z), name=name, in_specs=in_specs, out_shape=out_shape,
            out_specs=out_specs, scratch_shapes=scratch, compiler_params=PARAMS,
        )(*args)

    def exchange(x):
        n = x.shape[0]
        out = lax.all_to_all(x.reshape(n, 1, LANES), ("ray", "vox"), 0, 0, tiled=True)
        return out.reshape(n, LANES)

    tiles_v = pltpu.VMEM(tiles.shape, F32)
    per_ray = pltpu.VMEM((z.ray_blocks * LANES, LANES), F32)
    compact = pltpu.VMEM((z.compact, LANES), F32)
    sem = pltpu.SemaphoreType.DMA((z.slots // GROUP,))

    def middle(code, back, cols, name):
        return call(
            middle_kernel, name, [SMEM, VMEM, VMEM, ANY], (message, square, f32(8, LANES)),
            (VMEM, VMEM, VMEM), code, back, cols, tiles,
            scratch=(tiles_v, per_ray, compact, compact, per_ray, per_ray, sem),
        )

    msg, cols, code = call(
        first_kernel, "first", [SMEM, SMEM, SMEM, VMEM, ANY],
        (message, square, jax.ShapeDtypeStruct((z.slots,), jnp.int32)), (VMEM, VMEM, SMEM),
        tile_ray, tile_vox, tile_count, travel, tiles,
        scratch=(
            tiles_v, per_ray, compact, compact, pltpu.VMEM((LANES, LANES), F32),
            pltpu.SMEM((z.n_vox,), jnp.int32), sem,
        ),
    )
    n, m = z.data_rows * z.peers, z.segs * VBD
    back, y1, onehot, onehot_t = call(
        owner_first_kernel, "owner1", [VMEM],
        (message, owned, jax.ShapeDtypeStruct((m, n), BF16), jax.ShapeDtypeStruct((n, m), BF16)),
        (VMEM,) * 4, exchange(msg),
    )
    msg, cols, scal1 = middle(code, exchange(back), cols, "middle1")
    back, y2 = call(
        owner_next_kernel, "owner2", [VMEM] * 5, (message, owned), (VMEM,) * 2,
        exchange(msg), onehot, onehot_t, scal1, y1,
    )
    msg, cols, scal2 = middle(code, exchange(back), cols, "middle2")
    share, back = call(
        owner_last_kernel, "owner3", [VMEM] * 6, (f32(3 * VBD, LANES), f32(z.peers, LANES)),
        (VMEM,) * 2, exchange(msg), onehot, scal1, scal2, y1, y2,
    )
    shares = [share]
    hop = 1
    while hop < n_ray:
        pairs = [(r, r ^ hop) for r in range(n_ray)]
        shares = shares + [lax.ppermute(s, "ray", pairs) for s in shares]
        hop *= 2
    return call(
        final_kernel, "final", [VMEM] * (1 + n_ray), (owned, owned), (VMEM,) * 2,
        exchange(back), *shares,
    )


def solution(mesh):
    return jax.shard_map(
        on_device,
        mesh=mesh,
        in_specs=(
            P(("ray", "vox"), None, None),
            P(("ray", "vox")),
            P(("ray", "vox")),
            P(("ray", "vox")),
            P(("ray", "vox"), None),
        ),
        out_specs=(P("vox", None), P("vox", None)),
        check_vma=False,
    )
```

time: 526 us -> 82.1 us (0.16)
  blocking collectives: 271 us -> 60.2 us
  waiting for transfers between devices: 188 us -> 0.5 us
  matrix products: 35.5 us -> 0 us
  between operations: 19.1 us -> 1.33 us
  Pallas kernels: 0 us -> 13.8 us
  other arithmetic: 9.11 us -> 0 us
    psum x9 -> x0, blocking collectives: 209 us -> none  [the longest x3 116 us: ray_length(): return jnp.sqrt(lax.psum(jnp.sum(ray_vec * ray_vec), ('ray', 'vox')))]
    reduce_scatter x3 -> x0, waiting for transfers between devices: 188 us -> none  [backward(): lax.psum_scatter(partial_sum, 'vox', scatter_dimension=0, tiled=True)]
    all_gather x2 -> x0, blocking collectives: 62 us -> none  [on_device(): whole = lax.all_gather(vox_vec, 'vox', axis=0, tiled=True)]
    all_to_all x0 -> x6, blocking collectives: none -> 60.2 us  [exchange(): lax.all_to_all(x.reshape(n, 1, LANES), ('ray', 'vox'), 0, 0, tiled=True)]
    dot_general x10 -> x0, matrix products: 35.5 us -> none  [the longest x2 16.6 us: on_device(): jnp.einsum('tij,tj->ti', tiles, whole[tile_vox], precision=HIGH) * live]
    pallas_call x0 -> x7, Pallas kernels: none -> 13.8 us  [call(): pl.pallas_call(functools.partial(kernel, z), name=name, in_specs=in_specs...]
  transfers between devices with their start and end apart: 3 -> 3, of which waited for: 3 -> 1; matrix products, arithmetic and copies ran while one was open for 0% -> 0% of each run, Pallas kernels for 0% -> 0%
where the time goes in v1:
time: 82.1 us; the launch traced here: 81.7 us
  blocking collectives  60.2 us (73%)
  Pallas kernels  13.8 us (17%)
  local copies, waits for them, and re-layouts  4.19 us (5%)
  starting transfers between devices  1.72 us (2%)
  between operations  1.33 us (2%)
    all_to_all x6, blocking collectives, exchange(): lax.all_to_all(x.reshape(n, 1, LANES), ('ray', 'vox'), 0, 0, tiled=True)  60.2 us
    pallas_call x7, Pallas kernels, call(): pl.pallas_call(functools.partial(kernel, z), name=name, in_specs=in_specs...  13.8 us
    unnamed x10, local copies, waits for them, and re-layouts  4.19 us
    ppermute x3, starting transfers between devices, on_device(): shares = shares + [lax.ppermute(s, 'ray', pairs) for s in shares]  1.72 us
  transfers between devices with their start and end apart: 3, of which 1 were waited for; matrix products, arithmetic and copies ran while one was open for 0% of the time, Pallas kernels for 0%

profile of v1, /device:TPU:0, one launch (start us, length us, event | category | flops | bytes accessed | tf_op | source)
XLA Modules:
  0.0 81.7 jit_solution(12204047626374107503)
XLA Ops:
  1.3 2.2 %copy-done = f32[64,128,128]{2,1,0:T(8,128)S(1)} copy-done((f32[64,128,128]{2,1,0:T(8,128)S(1)}, f32[64,128,128]{2,1,0:T(8,128)}, u32[]{:S(2)}) %copy-start) | copy-done | bytes 4194328
  3.5 0.7 copy-done.2
  4.2 0.7 copy-done.3
  4.8 0.7 copy-done.4
  5.5 2.7 %first.1 = (f32[160,128]{1,0:T(8,128)S(1)}, f32[128,128]{1,0:T(8,128)S(1)}, s32[64]{0:T(128)S(1)}) custom-call(s32[64]{0:T(128)S(1)} %copy-done.3, s32[64]{0:T(128)S(1)} %copy-done.4, s32[1]{0:T(128)S(6)} %copy.13.tile_count, f32[16,128]{1,0:T(8,128)S(1)} %copy-done.2, f32[64,128,128]{2,1,0:T(8,128)S(1)} %copy-done), custom_call_target="tpu_custom_call" | custom-call | tf_op jit(solution)/shard_map/first/pallas_call | solution.py:329
  8.2 14.5 %all_to_all.30 = f32[160,1,128]{2,1,0:T(1,128)S(1)} all-to-all(f32[160,1,128]{2,1,0:T(1,128)S(1)} %bitcast.32), channel_id=1, replica_groups=mesh['ray'=4,'vox'=8] {'ray','vox'}, dimensions={0} | all-to-all | bytes 163840 | tf_op jit(solution)/shard_map/all_to_all | solution.py:336
  22.7 0.7 owner1.1
  23.5 9.1 %all_to_all.31 = f32[160,1,128]{2,1,0:T(1,128)S(1)} all-to-all(f32[160,1,128]{2,1,0:T(1,128)S(1)} %bitcast.30), channel_id=1, replica_groups=mesh['ray'=4,'vox'=8] {'ray','vox'}, dimensions={0} | all-to-all | bytes 163840 | tf_op jit(solution)/shard_map/all_to_all | solution.py:336
  32.6 0.0 copy-done.1
  32.6 4.1 %middle1.1 = (f32[160,128]{1,0:T(8,128)S(1)}, f32[128,128]{1,0:T(8,128)S(1)}, f32[8,128]{1,0:T(8,128)S(1)}) custom-call(s32[64]{0:T(128)S(1)} %get-tuple-element.18.code, f32[160,128]{1,0:T(8,128)S(1)} %bitcast.28, f32[128,128]{1,0:T(8,128)S(1)} %get-tuple-element.21.old_cols, f32[64,128,128]{2,1,0:T(8,128)S(1)} %copy-done.1), custom_call_target="tpu_custom_call" | custom-call | tf_op jit(solution)/shard_map/middle1/pallas_call | solution.py:329
  36.7 9.1 %all_to_all.32 = f32[160,1,128]{2,1,0:T(1,128)S(1)} all-to-all(f32[160,1,128]{2,1,0:T(1,128)S(1)} %bitcast.31), channel_id=1, replica_groups=mesh['ray'=4,'vox'=8] {'ray','vox'}, dimensions={0} | all-to-all | bytes 163840 | tf_op jit(solution)/shard_map/all_to_all | solution.py:336
  45.8 0.5 owner2.1
  46.4 9.1 %all_to_all.33 = f32[160,1,128]{2,1,0:T(1,128)S(1)} all-to-all(f32[160,1,128]{2,1,0:T(1,128)S(1)} %bitcast.33), channel_id=1, replica_groups=mesh['ray'=4,'vox'=8] {'ray','vox'}, dimensions={0} | all-to-all | bytes 163840 | tf_op jit(solution)/shard_map/all_to_all | solution.py:336
  55.5 4.6 %middle2.1 = (f32[160,128]{1,0:T(8,128)S(1)}, f32[128,128]{1,0:T(8,128)}, f32[8,128]{1,0:T(8,128)S(1)}) custom-call(s32[64]{0:T(128)S(1)} %get-tuple-element.18.code, f32[160,128]{1,0:T(8,128)S(1)} %bitcast.27, f32[128,128]{1,0:T(8,128)S(1)} %get-tuple-element.28.old_cols, f32[64,128,128]{2,1,0:T(8,128)S(1)} %copy-done.1), custom_call_target="tpu_custom_call" | custom-call | tf_op jit(solution)/shard_map/middle2/pallas_call | solution.py:329
  60.1 9.1 %all_to_all.34 = f32[160,1,128]{2,1,0:T(1,128)S(1)} all-to-all(f32[160,1,128]{2,1,0:T(1,128)S(1)} %bitcast.29), channel_id=1, replica_groups=mesh['ray'=4,'vox'=8] {'ray','vox'}, dimensions={0} | all-to-all | bytes 163840 | tf_op jit(solution)/shard_map/all_to_all | solution.py:336
  69.3 0.4 owner3.1
  69.7 0.2 collective-permute-start
  69.9 0.7 collective-permute-start.1
  70.6 0.5 collective-permute-done.refs_1_
  71.1 0.8 %collective-permute-start.2 = (f32[192,128]{1,0:T(8,128)S(1)}, f32[192,128]{1,0:T(8,128)S(1)}, u32[]{:S(2)}, u32[]{:S(2)}) collective-permute-start(f32[192,128]{1,0:T(8,128)S(1)} %collective-permute-done.refs_1_), channel_id=1, source_target_pairs={{0,16},{8,24},{16,0},{24,8},{1,17},{9,25},{17,1},{25,9},{2,18},{10... | collective-permute-start | bytes 294920 | tf_op jit(solution)/shard_map/ppermute | solution.py:380
  71.9 9.1 %all_to_all.35 = f32[32,1,128]{2,1,0:T(1,128)S(1)} all-to-all(f32[32,1,128]{2,1,0:T(1,128)S(1)} %bitcast.35), channel_id=1, replica_groups=mesh['ray'=4,'vox'=8] {'ray','vox'}, dimensions={0} | all-to-all | bytes 32768 | tf_op jit(solution)/shard_map/all_to_all | solution.py:336
  81.0 0.0 collective-permute-done.1.refs_2_
  81.0 0.0 collective-permute-done.2.refs_3_
  81.0 0.7 final.1
  (5 shorter events, 0.0 us)
Async XLA Ops:
  1.3 2.2 %copy-start = (f32[64,128,128]{2,1,0:T(8,128)S(1)}, f32[64,128,128]{2,1,0:T(8,128)}, u32[]{:S(2)}) copy-start(f32[64,128,128]{2,1,0:T(8,128)} %tiles_hbm.5) | copy-start | bytes 12582916
  3.5 0.7 copy-start.2
  4.2 0.7 copy-start.3
  4.8 0.7 copy-start.4
  5.5 27.1 %copy-start.1 = (f32[64,128,128]{2,1,0:T(8,128)S(1)}, f32[64,128,128]{2,1,0:T(8,128)}, u32[]{:S(2)}) copy-start(f32[64,128,128]{2,1,0:T(8,128)} %tiles_hbm.5) | copy-start | bytes 12582916
  69.7 1.4 %collective-permute-start = (f32[192,128]{1,0:T(8,128)S(1)}, f32[192,128]{1,0:T(8,128)S(1)}, u32[]{:S(2)}, u32[]{:S(2)}) collective-permute-start(f32[192,128]{1,0:T(8,128)S(1)} %get-tuple-element.33.refs_0_), channel_id=1, source_target_pairs={{0,8},{8,0},{16,24},{24,16},{1,9},{9,1},{17,25},{25,17},{2,10},{10... | collective-permute-start | bytes 294920 | tf_op jit(solution)/shard_map/ppermute | solution.py:380
  69.9 11.1 %collective-permute-start.1 = (f32[192,128]{1,0:T(8,128)S(1)}, f32[192,128]{1,0:T(8,128)S(1)}, u32[]{:S(2)}, u32[]{:S(2)}) collective-permute-start(f32[192,128]{1,0:T(8,128)S(1)} %get-tuple-element.33.refs_0_), channel_id=1, source_target_pairs={{0,16},{8,24},{16,0},{24,8},{1,17},{9,25},{17,1},{25,9},{2,18},{10... | collective-permute-start | bytes 294920 | tf_op jit(solution)/shard_map/ppermute | solution.py:380
  71.1 10.0 %collective-permute-start.2 = (f32[192,128]{1,0:T(8,128)S(1)}, f32[192,128]{1,0:T(8,128)S(1)}, u32[]{:S(2)}, u32[]{:S(2)}) collective-permute-start(f32[192,128]{1,0:T(8,128)S(1)} %collective-permute-done.refs_1_), channel_id=1, source_target_pairs={{0,16},{8,24},{16,0},{24,8},{1,17},{9,25},{17,1},{25,9},{2,18},{10... | collective-permute-start | bytes 294920 | tf_op jit(solution)/shard_map/ppermute | solution.py:380

commit v2 on v1

--- a/solution.py
+++ b/solution.py
@@ -10,6 +10,7 @@
 VBD = 64
 LANES = 128
 GROUP = 8
+AHEAD = 8
 F32 = jnp.float32
 BF16 = jnp.bfloat16
 
@@ -57,19 +58,9 @@
     return out[:, :width] + out[:, width : 2 * width] + out[:, 2 * width :]
 
 
-def tile_copies(tiles_hbm, tiles_v, sem, slots):
-    return [
-        pltpu.make_async_copy(
-            tiles_hbm.at[pl.ds(c * GROUP, GROUP)], tiles_v.at[pl.ds(c * GROUP, GROUP)], sem.at[c]
-        )
-        for c in range(slots // GROUP)
-    ]
-
-
-def wait_group(tiles_hbm, tiles_v, sem, c):
-    pltpu.make_async_copy(
-        tiles_hbm.at[pl.ds(c * GROUP, GROUP)], tiles_v.at[pl.ds(c * GROUP, GROUP)], sem.at[c]
-    ).wait()
+def tile_copy(tiles_hbm, tiles_v, sem, c):
+    part = pl.ds(c * GROUP, GROUP)
+    return pltpu.make_async_copy(tiles_hbm.at[part], tiles_v.at[part], sem.at[c])
 
 
 def write_products(z, prod, msg, meta):
@@ -89,68 +80,82 @@
         )
 
 
-def backward(z, where_of, tiles_v, rays_wide, prod, wait):
+def backward(z, where_of, tiles_v, wide, prod, ready=None):
     def step(c, carry):
-        if wait is not None:
-            wait(c)
+        if ready is not None:
+            ready(c)
         for s in range(GROUP):
             t = c * GROUP + s
             ray, row = where_of(t)
-            block = rays_wide[pl.ds(ray * LANES, LANES), :]
-            prod[pl.ds(row, 1), :] = jnp.sum(tiles_v[t] * block, axis=0, keepdims=True)
+            prod[pl.ds(row, 1), :] = jnp.sum(tiles_v[t] * wide[ray], axis=0, keepdims=True)
         return carry
 
     lax.fori_loop(0, z.slots // GROUP, step, 0)
 
 
 def first_kernel(
-    z, tile_ray, tile_vox, tile_count, travel, tiles_hbm, msg, cols, code,
-    tiles_v, rays_wide, prod, named, pad, count, sem,
+    z, ray_hbm, vox_hbm, tile_count, travel_hbm, tiles_hbm, msg, wide, code_out, tiles_v,
+    prod, named, pad, tile_ray, tile_vox, travel, code, count, sem, small_sem, code_sem,
 ):
-    for copy in tile_copies(tiles_hbm, tiles_v, sem, z.slots):
+    small = [
+        pltpu.make_async_copy(src, dst, small_sem.at[i])
+        for i, (src, dst) in enumerate(
+            [(ray_hbm, tile_ray), (vox_hbm, tile_vox), (travel_hbm, travel)]
+        )
+    ]
+    groups = z.slots // GROUP
+    for copy in small:
         copy.start()
+    for c in range(min(AHEAD, groups)):
+        tile_copy(tiles_hbm, tiles_v, sem, c).start()
     for o in range(z.n_vox):
         count[o] = 0
     prod[...] = jnp.zeros_like(prod)
     named[...] = jnp.full_like(named, -1.0)
     pad[...] = jnp.zeros_like(pad)
+    for copy in small:
+        copy.wait()
     pad[pl.ds(0, z.ray_blocks), :] = travel[...]
     by_col = pad[...].T
-    cols[...] = by_col
     for r in range(z.ray_blocks):
-        rays_wide[pl.ds(r * LANES, LANES), :] = jnp.broadcast_to(
-            by_col[:, r : r + 1], (LANES, LANES)
-        )
+        wide[r] = jnp.broadcast_to(by_col[:, r : r + 1], (LANES, LANES))
     live = tile_count[0]
+
+    def ready(c):
+        tile_copy(tiles_hbm, tiles_v, sem, c).wait()
+
+        @pl.when(c + AHEAD < groups)
+        def _():
+            tile_copy(tiles_hbm, tiles_v, sem, c + AHEAD).start()
 
     def where_of(t):
         vox, ray = tile_vox[t], tile_ray[t]
-        owner = vox // VBD
+        owner = lax.shift_right_logical(vox, VBD.bit_length() - 1)
         k = count[owner]
         count[owner] = k + 1
         row = k * z.n_vox + owner
         code[t] = row * 256 + ray
-        block = jnp.where(t < live, vox - owner * VBD, -1).astype(F32)
+        block = jnp.where(t < live, vox & (VBD - 1), -1).astype(F32)
         named[pl.ds(row, 1), :] = jnp.full((1, LANES), block, F32)
         return ray, row
 
-    backward(
-        z, where_of, tiles_v, rays_wide, prod,
-        lambda c: wait_group(tiles_hbm, tiles_v, sem, c),
-    )
+    backward(z, where_of, tiles_v, wide, prod, ready)
+    keep = pltpu.make_async_copy(code, code_out, code_sem)
+    keep.start()
     here = lane((z.n_vox, LANES))
     meta = jnp.where(here == z.cap, total(travel[...] * travel[...]), 0.0)
     for k in range(z.cap):
         meta = jnp.where(here == k, named[pl.ds(k * z.n_vox, z.n_vox), :], meta)
     write_products(z, prod, msg, meta)
+    keep.wait()
 
 
 def middle_kernel(
-    z, code, back, old_cols, tiles_hbm, msg, cols, scal,
-    tiles_v, rays_wide, prod, vox_rows, sums, sems, sem,
+    z, code_v, back, old, tiles_v, msg, scal, *refs
 ):
-    for copy in tile_copies(tiles_hbm, tiles_v, sem, z.slots):
-        copy.start()
+    wide, prod, vox_rows, sums, sems, code, code_sem = refs
+    fetch = pltpu.make_async_copy(code_v, code, code_sem)
+    fetch.start()
     meta = back[pl.ds(z.data_rows, z.peers, stride=z.rows), :]
     alpha = jnp.sqrt(pick(jnp.sum(meta, axis=0, keepdims=True), 0))
     beta = pick(meta[0:1], 1)
@@ -167,36 +172,37 @@
             for r in range(z.n_ray):
                 row = jnp.where(segment == r, shift_lanes(part[r], (r - g) * z.seg), row)
             vox_rows[pl.ds((q * z.segs + g) * z.n_vox, z.n_vox), :] = row / alpha
-    sums[...] = jnp.zeros_like(sums)
-    sems[...] = jnp.zeros_like(sems)
+    lane_share = -alpha / beta * (1.0 / LANES)
+    for r in range(z.ray_blocks):
+        sums[r] = old[r] * lane_share
+        sems[r] = jnp.zeros((LANES, LANES), F32)
     prod[...] = jnp.zeros_like(prod)
+    fetch.wait()
 
     def where_of(t):
         both = code[t]
-        return both & 255, both // 256
+        return both & 255, lax.shift_right_logical(both, 8)
 
     def step(c, carry):
-        wait_group(tiles_hbm, tiles_v, sem, c)
         for s in range(GROUP):
             t = c * GROUP + s
             ray, row = where_of(t)
             into = sums if s % 2 == 0 else sems
-            into[pl.ds(ray * LANES, LANES), :] += tiles_v[t] * vox_rows[pl.ds(row, 1), :]
+            into[ray] += tiles_v[t] * vox_rows[pl.ds(row, 1), :]
         return carry
 
     lax.fori_loop(0, z.slots // GROUP, step, 0)
-    at = lane((LANES, LANES))
-    before = old_cols[...] / beta
-    now = jnp.zeros((LANES, LANES), F32)
+    square = jnp.zeros((LANES, LANES), F32)
     for r in range(z.ray_blocks):
-        both = sums[pl.ds(r * LANES, LANES), :] + sems[pl.ds(r * LANES, LANES), :]
-        u = jnp.sum(both, axis=1, keepdims=True) - alpha * before[:, r : r + 1]
-        wide = jnp.broadcast_to(u, (LANES, LANES))
-        rays_wide[pl.ds(r * LANES, LANES), :] = wide
-        now = jnp.where(at == r, wide, now)
-    cols[...] = now
-    backward(z, where_of, tiles_v, rays_wide, prod, None)
-    meta = jnp.where(lane((z.n_vox, LANES)) == z.cap, total(now * now), 0.0)
+        u = jnp.broadcast_to(
+            jnp.sum(sums[r] + sems[r], axis=1, keepdims=True), (LANES, LANES)
+        )
+        wide[r] = u
+        square += u * u
+    backward(z, where_of, tiles_v, wide, prod)
+    meta = jnp.where(
+        lane((z.n_vox, LANES)) == z.cap, total(square) * (1.0 / LANES), 0.0
+    )
     write_products(z, prod, msg, meta)
 
 
@@ -310,8 +316,12 @@
 
 SMEM = pl.BlockSpec(memory_space=pltpu.SMEM)
 VMEM = pl.BlockSpec(memory_space=pltpu.VMEM)
-ANY = pl.BlockSpec(memory_space=pl.ANY)
+HBM = pl.BlockSpec(memory_space=pltpu.HBM)
 PARAMS = pltpu.CompilerParams(vmem_limit_bytes=24 * 1024 * 1024)
+
+
+def in_hbm(x):
+    return pltpu.with_memory_space_constraint(x, pltpu.HBM)
 
 
 def f32(*shape):
@@ -322,7 +332,7 @@
     n_ray, n_vox = lax.axis_size("ray"), lax.axis_size("vox")
     z = Sizes(n_ray, n_vox, tiles.shape[0], travel.shape[0])
     message = f32(z.peers * z.rows, LANES)
-    square = f32(LANES, LANES)
+    wide_rays = f32(z.ray_blocks, LANES, LANES)
     owned = f32(VBD, LANES)
 
     def call(kernel, name, in_specs, out_shape, out_specs, *args, scratch=()):
@@ -336,25 +346,29 @@
         out = lax.all_to_all(x.reshape(n, 1, LANES), ("ray", "vox"), 0, 0, tiled=True)
         return out.reshape(n, LANES)
 
-    tiles_v = pltpu.VMEM(tiles.shape, F32)
-    per_ray = pltpu.VMEM((z.ray_blocks * LANES, LANES), F32)
+    per_ray = pltpu.VMEM((z.ray_blocks, LANES, LANES), F32)
     compact = pltpu.VMEM((z.compact, LANES), F32)
-    sem = pltpu.SemaphoreType.DMA((z.slots // GROUP,))
-
-    def middle(code, back, cols, name):
+    indices = pltpu.SMEM((z.slots,), jnp.int32)
+    one_sem = pltpu.SemaphoreType.DMA(())
+
+    def middle(back, wide, last):
+        scratch = (compact, compact, per_ray, per_ray, indices, one_sem)
+        out = (message, f32(8, LANES))
         return call(
-            middle_kernel, name, [SMEM, VMEM, VMEM, ANY], (message, square, f32(8, LANES)),
-            (VMEM, VMEM, VMEM), code, back, cols, tiles,
-            scratch=(tiles_v, per_ray, compact, compact, per_ray, per_ray, sem),
+            middle_kernel, "middle2" if last else "middle1", (VMEM,) * 4,
+            out if last else out + (wide_rays,), (VMEM,) * (2 if last else 3),
+            code, back, wide, tiles_v, scratch=(per_ray,) + scratch if last else scratch,
         )
 
-    msg, cols, code = call(
-        first_kernel, "first", [SMEM, SMEM, SMEM, VMEM, ANY],
-        (message, square, jax.ShapeDtypeStruct((z.slots,), jnp.int32)), (VMEM, VMEM, SMEM),
-        tile_ray, tile_vox, tile_count, travel, tiles,
+    msg, wide, code, tiles_v = call(
+        first_kernel, "first", [HBM, HBM, SMEM, HBM, HBM],
+        (message, wide_rays, jax.ShapeDtypeStruct((z.slots,), jnp.int32), f32(*tiles.shape)),
+        (VMEM,) * 4,
+        in_hbm(tile_ray), in_hbm(tile_vox), tile_count, in_hbm(travel), in_hbm(tiles),
         scratch=(
-            tiles_v, per_ray, compact, compact, pltpu.VMEM((LANES, LANES), F32),
-            pltpu.SMEM((z.n_vox,), jnp.int32), sem,
+            compact, compact, pltpu.VMEM((LANES, LANES), F32), indices, indices,
+            pltpu.VMEM(travel.shape, F32), indices, pltpu.SMEM((z.n_vox,), jnp.int32),
+            pltpu.SemaphoreType.DMA((z.slots // GROUP,)), pltpu.SemaphoreType.DMA((3,)), one_sem,
         ),
     )
     n, m = z.data_rows * z.peers, z.segs * VBD
@@ -363,12 +377,12 @@
         (message, owned, jax.ShapeDtypeStruct((m, n), BF16), jax.ShapeDtypeStruct((n, m), BF16)),
         (VMEM,) * 4, exchange(msg),
     )
-    msg, cols, scal1 = middle(code, exchange(back), cols, "middle1")
+    msg, scal1, wide = middle(exchange(back), wide, False)
     back, y2 = call(
         owner_next_kernel, "owner2", [VMEM] * 5, (message, owned), (VMEM,) * 2,
         exchange(msg), onehot, onehot_t, scal1, y1,
     )
-    msg, cols, scal2 = middle(code, exchange(back), cols, "middle2")
+    msg, scal2 = middle(exchange(back), wide, True)
     share, back = call(
         owner_last_kernel, "owner3", [VMEM] * 6, (f32(3 * VBD, LANES), f32(z.peers, LANES)),
         (VMEM,) * 2, exchange(msg), onehot, scal1, scal2, y1, y2,

time: 82.1 us -> 74.3 us (0.905)
  local copies, waits for them, and re-layouts: 4.19 us -> 0 us
  Pallas kernels: 13.8 us -> 10.3 us
    unnamed x10 -> x0, local copies, waits for them, and re-layouts: 4.19 us -> none
    pallas_call x7, Pallas kernels: 13.8 us -> 10.3 us  [call(): pl.pallas_call(functools.partial(kernel, z), name=name, in_specs=in_specs...]
where the time goes in v2:
time: 74.3 us; the launch traced here: 74 us
  blocking collectives  60.1 us (81%)
  Pallas kernels  10.3 us (14%)
  starting transfers between devices  1.75 us (2%)
  between operations  1.32 us (2%)
    all_to_all x6, blocking collectives, exchange(): lax.all_to_all(x.reshape(n, 1, LANES), ('ray', 'vox'), 0, 0, tiled=True)  60.1 us
    pallas_call x7, Pallas kernels, call(): pl.pallas_call(functools.partial(kernel, z), name=name, in_specs=in_specs...  10.3 us
    ppermute x3, starting transfers between devices, on_device(): shares = shares + [lax.ppermute(s, 'ray', pairs) for s in shares]  1.75 us
  transfers between devices with their start and end apart: 3, of which 1 were waited for; matrix products, arithmetic and copies ran while one was open for 0% of the time, Pallas kernels for 0%

profile of v2, /device:TPU:0, one launch (start us, length us, event | category | flops | bytes accessed | tf_op | source)
XLA Modules:
  0.0 74.0 jit_solution(2408451584851374457)
XLA Ops:
  1.3 3.6 %first.1 = (f32[160,128]{1,0:T(8,128)S(1)}, f32[16,128,128]{2,1,0:T(8,128)S(1)}, s32[64]{0:T(128)S(1)}, f32[64,128,128]{2,1,0:T(8,128)S(1)}) custom-call(s32[64]{0:T(128)} %ray_hbm.1, s32[64]{0:T(128)} %vox_hbm.1, s32[1]{0:T(128)S(6)} %copy.13.tile_count, f32[16,128]{1,0:T(8,128)} %travel_hbm.1, f32[64,128,128]{2,1,0:T(8,128)} %tiles_hbm.1), custom_call_target="tpu_custom_call" | custom-call | tf_op jit(solution)/shard_map/first/pallas_call | solution.py:339
  4.9 14.5 %all_to_all.30 = f32[160,1,128]{2,1,0:T(1,128)S(1)} all-to-all(f32[160,1,128]{2,1,0:T(1,128)S(1)} %bitcast.30), channel_id=1, replica_groups=mesh['ray'=4,'vox'=8] {'ray','vox'}, dimensions={0} | all-to-all | bytes 163840 | tf_op jit(solution)/shard_map/all_to_all | solution.py:346
  19.4 0.7 owner1.1
  20.1 9.1 %all_to_all.31 = f32[160,1,128]{2,1,0:T(1,128)S(1)} all-to-all(f32[160,1,128]{2,1,0:T(1,128)S(1)} %bitcast.31), channel_id=1, replica_groups=mesh['ray'=4,'vox'=8] {'ray','vox'}, dimensions={0} | all-to-all | bytes 163840 | tf_op jit(solution)/shard_map/all_to_all | solution.py:346
  29.3 2.1 %middle1.1 = (f32[160,128]{1,0:T(8,128)S(1)}, f32[8,128]{1,0:T(8,128)S(1)}, f32[16,128,128]{2,1,0:T(8,128)S(1)}) custom-call(s32[64]{0:T(128)S(1)} %get-tuple-element.19.code_v, f32[160,128]{1,0:T(8,128)S(1)} %bitcast.28, f32[16,128,128]{2,1,0:T(8,128)S(1)} %get-tuple-element.22.old, f32[64,128,128]{2,1,0:T(8,128)S(1)} %get-tuple-element.23.tiles_v), custom_call_target="tpu_custom_call" | custom-call | tf_op jit(solution)/shard_map/middle1/pallas_call | solution.py:339
  31.4 9.1 %all_to_all.32 = f32[160,1,128]{2,1,0:T(1,128)S(1)} all-to-all(f32[160,1,128]{2,1,0:T(1,128)S(1)} %bitcast.32), channel_id=1, replica_groups=mesh['ray'=4,'vox'=8] {'ray','vox'}, dimensions={0} | all-to-all | bytes 163840 | tf_op jit(solution)/shard_map/all_to_all | solution.py:346
  40.5 0.5 owner2.1
  41.0 9.1 %all_to_all.33 = f32[160,1,128]{2,1,0:T(1,128)S(1)} all-to-all(f32[160,1,128]{2,1,0:T(1,128)S(1)} %bitcast.33), channel_id=1, replica_groups=mesh['ray'=4,'vox'=8] {'ray','vox'}, dimensions={0} | all-to-all | bytes 163840 | tf_op jit(solution)/shard_map/all_to_all | solution.py:346
  50.2 2.2 %middle2.1 = (f32[160,128]{1,0:T(8,128)S(1)}, f32[8,128]{1,0:T(8,128)S(1)}) custom-call(s32[64]{0:T(128)S(1)} %get-tuple-element.19.code_v, f32[160,128]{1,0:T(8,128)S(1)} %bitcast.27, f32[16,128,128]{2,1,0:T(8,128)S(1)} %get-tuple-element.30.old, f32[64,128,128]{2,1,0:T(8,128)S(1)} %get-tuple-element.23.tiles_v), custom_call_target="tpu_custom_call" | custom-call | tf_op jit(solution)/shard_map/middle2/pallas_call | solution.py:339
  52.4 9.1 %all_to_all.34 = f32[160,1,128]{2,1,0:T(1,128)S(1)} all-to-all(f32[160,1,128]{2,1,0:T(1,128)S(1)} %bitcast.29), channel_id=1, replica_groups=mesh['ray'=4,'vox'=8] {'ray','vox'}, dimensions={0} | all-to-all | bytes 163840 | tf_op jit(solution)/shard_map/all_to_all | solution.py:346
  61.5 0.4 owner3.1
  62.0 0.2 collective-permute-start
  62.2 0.7 collective-permute-start.1
  62.8 0.5 collective-permute-done.refs_1_
  63.3 0.9 %collective-permute-start.2 = (f32[192,128]{1,0:T(8,128)S(1)}, f32[192,128]{1,0:T(8,128)S(1)}, u32[]{:S(2)}, u32[]{:S(2)}) collective-permute-start(f32[192,128]{1,0:T(8,128)S(1)} %collective-permute-done.refs_1_), channel_id=1, source_target_pairs={{0,16},{8,24},{16,0},{24,8},{1,17},{9,25},{17,1},{25,9},{2,18},{10... | collective-permute-start | bytes 294920 | tf_op jit(solution)/shard_map/ppermute | solution.py:394
  64.2 9.1 %all_to_all.35 = f32[32,1,128]{2,1,0:T(1,128)S(1)} all-to-all(f32[32,1,128]{2,1,0:T(1,128)S(1)} %bitcast.35), channel_id=1, replica_groups=mesh['ray'=4,'vox'=8] {'ray','vox'}, dimensions={0} | all-to-all | bytes 32768 | tf_op jit(solution)/shard_map/all_to_all | solution.py:346
  73.3 0.0 collective-permute-done.1.refs_2_
  73.3 0.0 collective-permute-done.2.refs_3_
  73.3 0.7 final.1
Async XLA Ops:
  62.0 1.4 %collective-permute-start = (f32[192,128]{1,0:T(8,128)S(1)}, f32[192,128]{1,0:T(8,128)S(1)}, u32[]{:S(2)}, u32[]{:S(2)}) collective-permute-start(f32[192,128]{1,0:T(8,128)S(1)} %get-tuple-element.35.refs_0_), channel_id=1, source_target_pairs={{0,8},{8,0},{16,24},{24,16},{1,9},{9,1},{17,25},{25,17},{2,10},{10... | collective-permute-start | bytes 294920 | tf_op jit(solution)/shard_map/ppermute | solution.py:394
  62.2 11.1 %collective-permute-start.1 = (f32[192,128]{1,0:T(8,128)S(1)}, f32[192,128]{1,0:T(8,128)S(1)}, u32[]{:S(2)}, u32[]{:S(2)}) collective-permute-start(f32[192,128]{1,0:T(8,128)S(1)} %get-tuple-element.35.refs_0_), channel_id=1, source_target_pairs={{0,16},{8,24},{16,0},{24,8},{1,17},{9,25},{17,1},{25,9},{2,18},{10... | collective-permute-start | bytes 294920 | tf_op jit(solution)/shard_map/ppermute | solution.py:394
  63.3 9.9 %collective-permute-start.2 = (f32[192,128]{1,0:T(8,128)S(1)}, f32[192,128]{1,0:T(8,128)S(1)}, u32[]{:S(2)}, u32[]{:S(2)}) collective-permute-start(f32[192,128]{1,0:T(8,128)S(1)} %collective-permute-done.refs_1_), channel_id=1, source_target_pairs={{0,16},{8,24},{16,0},{24,8},{1,17},{9,25},{17,1},{25,9},{2,18},{10... | collective-permute-start | bytes 294920 | tf_op jit(solution)/shard_map/ppermute | solution.py:394

commit v3 on v2

--- a/solution.py
+++ b/solution.py
@@ -10,7 +10,6 @@
 VBD = 64
 LANES = 128
 GROUP = 8
-AHEAD = 8
 F32 = jnp.float32
 BF16 = jnp.bfloat16
 
@@ -80,7 +79,7 @@
         )
 
 
-def backward(z, where_of, tiles_v, wide, prod, ready=None):
+def backward(groups, where_of, tiles_v, wide, prod, ready=None):
     def step(c, carry):
         if ready is not None:
             ready(c)
@@ -90,7 +89,7 @@
             prod[pl.ds(row, 1), :] = jnp.sum(tiles_v[t] * wide[ray], axis=0, keepdims=True)
         return carry
 
-    lax.fori_loop(0, z.slots // GROUP, step, 0)
+    lax.fori_loop(0, groups, step, 0)
 
 
 def first_kernel(
@@ -100,33 +99,34 @@
     small = [
         pltpu.make_async_copy(src, dst, small_sem.at[i])
         for i, (src, dst) in enumerate(
-            [(ray_hbm, tile_ray), (vox_hbm, tile_vox), (travel_hbm, travel)]
+            [(travel_hbm, travel), (ray_hbm, tile_ray), (vox_hbm, tile_vox)]
         )
     ]
-    groups = z.slots // GROUP
+    live = tile_count[0]
+    groups = lax.shift_right_logical(live + (GROUP - 1), GROUP.bit_length() - 1)
     for copy in small:
         copy.start()
-    for c in range(min(AHEAD, groups)):
-        tile_copy(tiles_hbm, tiles_v, sem, c).start()
+    for c in range(z.slots // GROUP):
+
+        @pl.when(c < groups)
+        def _():
+            tile_copy(tiles_hbm, tiles_v, sem, c).start()
+
     for o in range(z.n_vox):
         count[o] = 0
     prod[...] = jnp.zeros_like(prod)
     named[...] = jnp.full_like(named, -1.0)
     pad[...] = jnp.zeros_like(pad)
-    for copy in small:
-        copy.wait()
+    small[0].wait()
     pad[pl.ds(0, z.ray_blocks), :] = travel[...]
     by_col = pad[...].T
     for r in range(z.ray_blocks):
         wide[r] = jnp.broadcast_to(by_col[:, r : r + 1], (LANES, LANES))
-    live = tile_count[0]
+    for copy in small[1:]:
+        copy.wait()
 
     def ready(c):
         tile_copy(tiles_hbm, tiles_v, sem, c).wait()
-
-        @pl.when(c + AHEAD < groups)
-        def _():
-            tile_copy(tiles_hbm, tiles_v, sem, c + AHEAD).start()
 
     def where_of(t):
         vox, ray = tile_vox[t], tile_ray[t]
@@ -139,7 +139,8 @@
         named[pl.ds(row, 1), :] = jnp.full((1, LANES), block, F32)
         return ray, row
 
-    backward(z, where_of, tiles_v, wide, prod, ready)
+    code[z.slots] = groups
+    backward(groups, where_of, tiles_v, wide, prod, ready)
     keep = pltpu.make_async_copy(code, code_out, code_sem)
     keep.start()
     here = lane((z.n_vox, LANES))
@@ -178,6 +179,7 @@
         sems[r] = jnp.zeros((LANES, LANES), F32)
     prod[...] = jnp.zeros_like(prod)
     fetch.wait()
+    groups = code[z.slots]
 
     def where_of(t):
         both = code[t]
@@ -191,7 +193,7 @@
             into[ray] += tiles_v[t] * vox_rows[pl.ds(row, 1), :]
         return carry
 
-    lax.fori_loop(0, z.slots // GROUP, step, 0)
+    lax.fori_loop(0, groups, step, 0)
     square = jnp.zeros((LANES, LANES), F32)
     for r in range(z.ray_blocks):
         u = jnp.broadcast_to(
@@ -199,7 +201,7 @@
         )
         wide[r] = u
         square += u * u
-    backward(z, where_of, tiles_v, wide, prod)
+    backward(groups, where_of, tiles_v, wide, prod)
     meta = jnp.where(
         lane((z.n_vox, LANES)) == z.cap, total(square) * (1.0 / LANES), 0.0
     )
@@ -349,10 +351,11 @@
     per_ray = pltpu.VMEM((z.ray_blocks, LANES, LANES), F32)
     compact = pltpu.VMEM((z.compact, LANES), F32)
     indices = pltpu.SMEM((z.slots,), jnp.int32)
+    codes = pltpu.SMEM((z.slots + 1,), jnp.int32)
     one_sem = pltpu.SemaphoreType.DMA(())
 
     def middle(back, wide, last):
-        scratch = (compact, compact, per_ray, per_ray, indices, one_sem)
+        scratch = (compact, compact, per_ray, per_ray, codes, one_sem)
         out = (message, f32(8, LANES))
         return call(
             middle_kernel, "middle2" if last else "middle1", (VMEM,) * 4,
@@ -362,12 +365,12 @@
 
     msg, wide, code, tiles_v = call(
         first_kernel, "first", [HBM, HBM, SMEM, HBM, HBM],
-        (message, wide_rays, jax.ShapeDtypeStruct((z.slots,), jnp.int32), f32(*tiles.shape)),
+        (message, wide_rays, jax.ShapeDtypeStruct((z.slots + 1,), jnp.int32), f32(*tiles.shape)),
         (VMEM,) * 4,
         in_hbm(tile_ray), in_hbm(tile_vox), tile_count, in_hbm(travel), in_hbm(tiles),
         scratch=(
             compact, compact, pltpu.VMEM((LANES, LANES), F32), indices, indices,
-            pltpu.VMEM(travel.shape, F32), indices, pltpu.SMEM((z.n_vox,), jnp.int32),
+            pltpu.VMEM(travel.shape, F32), codes, pltpu.SMEM((z.n_vox,), jnp.int32),
             pltpu.SemaphoreType.DMA((z.slots // GROUP,)), pltpu.SemaphoreType.DMA((3,)), one_sem,
         ),
     )

time: 74.3 us -> 72.7 us (0.978)
  Pallas kernels: 10.3 us -> 7.44 us
  blocking collectives: 60.1 us -> 61.5 us
    pallas_call x7, Pallas kernels: 10.3 us -> 7.44 us  [call(): pl.pallas_call(functools.partial(kernel, z), name=name, in_specs=in_specs...]
    all_to_all x6, blocking collectives: 60.1 us -> 61.5 us  [exchange(): lax.all_to_all(x.reshape(n, 1, LANES), ('ray', 'vox'), 0, 0, tiled=True)]
where the time goes in v3:
time: 72.7 us; the launch traced here: 72.5 us
  blocking collectives  61.5 us (85%)
  Pallas kernels  7.44 us (10%)
  starting transfers between devices  1.75 us (2%)
  between operations  1.32 us (2%)
    all_to_all x6, blocking collectives, exchange(): lax.all_to_all(x.reshape(n, 1, LANES), ('ray', 'vox'), 0, 0, tiled=True)  61.5 us
    pallas_call x7, Pallas kernels, call(): pl.pallas_call(functools.partial(kernel, z), name=name, in_specs=in_specs...  7.44 us
    ppermute x3, starting transfers between devices, on_device(): shares = shares + [lax.ppermute(s, 'ray', pairs) for s in shares]  1.75 us
  transfers between devices with their start and end apart: 3, of which 1 were waited for; matrix products, arithmetic and copies ran while one was open for 0% of the time, Pallas kernels for 0%

profile of v3, /device:TPU:0, one launch (start us, length us, event | category | flops | bytes accessed | tf_op | source)
XLA Modules:
  0.0 72.5 jit_solution(7961374603667248934)
XLA Ops:
  1.3 2.4 %first.1 = (f32[160,128]{1,0:T(8,128)S(1)}, f32[16,128,128]{2,1,0:T(8,128)S(1)}, s32[65]{0:T(128)S(1)}, f32[64,128,128]{2,1,0:T(8,128)S(1)}) custom-call(s32[64]{0:T(128)} %ray_hbm.1, s32[64]{0:T(128)} %vox_hbm.1, s32[1]{0:T(128)S(6)} %copy.13.tile_count, f32[16,128]{1,0:T(8,128)} %travel_hbm.1, f32[64,128,128]{2,1,0:T(8,128)} %tiles_hbm.1), custom_call_target="tpu_custom_call" | custom-call | tf_op jit(solution)/shard_map/first/pallas_call | solution.py:341
  3.7 15.4 %all_to_all.30 = f32[160,1,128]{2,1,0:T(1,128)S(1)} all-to-all(f32[160,1,128]{2,1,0:T(1,128)S(1)} %bitcast.30), channel_id=1, replica_groups=mesh['ray'=4,'vox'=8] {'ray','vox'}, dimensions={0} | all-to-all | bytes 163840 | tf_op jit(solution)/shard_map/all_to_all | solution.py:348
  19.0 0.7 owner1.1
  19.7 9.1 %all_to_all.31 = f32[160,1,128]{2,1,0:T(1,128)S(1)} all-to-all(f32[160,1,128]{2,1,0:T(1,128)S(1)} %bitcast.31), channel_id=1, replica_groups=mesh['ray'=4,'vox'=8] {'ray','vox'}, dimensions={0} | all-to-all | bytes 163840 | tf_op jit(solution)/shard_map/all_to_all | solution.py:348
  28.9 1.3 %middle1.1 = (f32[160,128]{1,0:T(8,128)S(1)}, f32[8,128]{1,0:T(8,128)S(1)}, f32[16,128,128]{2,1,0:T(8,128)S(1)}) custom-call(s32[65]{0:T(128)S(1)} %get-tuple-element.19.code_v, f32[160,128]{1,0:T(8,128)S(1)} %bitcast.28, f32[16,128,128]{2,1,0:T(8,128)S(1)} %get-tuple-element.22.old, f32[64,128,128]{2,1,0:T(8,128)S(1)} %get-tuple-element.23.tiles_v), custom_call_target="tpu_custom_call" | custom-call | tf_op jit(solution)/shard_map/middle1/pallas_call | solution.py:341
  30.2 9.3 %all_to_all.32 = f32[160,1,128]{2,1,0:T(1,128)S(1)} all-to-all(f32[160,1,128]{2,1,0:T(1,128)S(1)} %bitcast.32), channel_id=1, replica_groups=mesh['ray'=4,'vox'=8] {'ray','vox'}, dimensions={0} | all-to-all | bytes 163840 | tf_op jit(solution)/shard_map/all_to_all | solution.py:348
  39.5 0.5 owner2.1
  40.0 9.1 %all_to_all.33 = f32[160,1,128]{2,1,0:T(1,128)S(1)} all-to-all(f32[160,1,128]{2,1,0:T(1,128)S(1)} %bitcast.33), channel_id=1, replica_groups=mesh['ray'=4,'vox'=8] {'ray','vox'}, dimensions={0} | all-to-all | bytes 163840 | tf_op jit(solution)/shard_map/all_to_all | solution.py:348
  49.1 1.4 %middle2.1 = (f32[160,128]{1,0:T(8,128)S(1)}, f32[8,128]{1,0:T(8,128)S(1)}) custom-call(s32[65]{0:T(128)S(1)} %get-tuple-element.19.code_v, f32[160,128]{1,0:T(8,128)S(1)} %bitcast.27, f32[16,128,128]{2,1,0:T(8,128)S(1)} %get-tuple-element.30.old, f32[64,128,128]{2,1,0:T(8,128)S(1)} %get-tuple-element.23.tiles_v), custom_call_target="tpu_custom_call" | custom-call | tf_op jit(solution)/shard_map/middle2/pallas_call | solution.py:341
  50.5 9.4 %all_to_all.34 = f32[160,1,128]{2,1,0:T(1,128)S(1)} all-to-all(f32[160,1,128]{2,1,0:T(1,128)S(1)} %bitcast.29), channel_id=1, replica_groups=mesh['ray'=4,'vox'=8] {'ray','vox'}, dimensions={0} | all-to-all | bytes 163840 | tf_op jit(solution)/shard_map/all_to_all | solution.py:348
  59.9 0.4 owner3.1
  60.4 0.2 collective-permute-start
  60.5 0.7 collective-permute-start.1
  61.2 0.5 collective-permute-done.refs_1_
  61.7 0.9 %collective-permute-start.2 = (f32[192,128]{1,0:T(8,128)S(1)}, f32[192,128]{1,0:T(8,128)S(1)}, u32[]{:S(2)}, u32[]{:S(2)}) collective-permute-start(f32[192,128]{1,0:T(8,128)S(1)} %collective-permute-done.refs_1_), channel_id=1, source_target_pairs={{0,16},{8,24},{16,0},{24,8},{1,17},{9,25},{17,1},{25,9},{2,18},{10... | collective-permute-start | bytes 294920 | tf_op jit(solution)/shard_map/ppermute | solution.py:397
  62.6 9.2 %all_to_all.35 = f32[32,1,128]{2,1,0:T(1,128)S(1)} all-to-all(f32[32,1,128]{2,1,0:T(1,128)S(1)} %bitcast.35), channel_id=1, replica_groups=mesh['ray'=4,'vox'=8] {'ray','vox'}, dimensions={0} | all-to-all | bytes 32768 | tf_op jit(solution)/shard_map/all_to_all | solution.py:348
  71.8 0.0 collective-permute-done.1.refs_2_
  71.8 0.0 collective-permute-done.2.refs_3_
  71.8 0.7 final.1
Async XLA Ops:
  60.4 1.4 %collective-permute-start = (f32[192,128]{1,0:T(8,128)S(1)}, f32[192,128]{1,0:T(8,128)S(1)}, u32[]{:S(2)}, u32[]{:S(2)}) collective-permute-start(f32[192,128]{1,0:T(8,128)S(1)} %get-tuple-element.35.refs_0_), channel_id=1, source_target_pairs={{0,8},{8,0},{16,24},{24,16},{1,9},{9,1},{17,25},{25,17},{2,10},{10... | collective-permute-start | bytes 294920 | tf_op jit(solution)/shard_map/ppermute | solution.py:397
  60.5 11.2 %collective-permute-start.1 = (f32[192,128]{1,0:T(8,128)S(1)}, f32[192,128]{1,0:T(8,128)S(1)}, u32[]{:S(2)}, u32[]{:S(2)}) collective-permute-start(f32[192,128]{1,0:T(8,128)S(1)} %get-tuple-element.35.refs_0_), channel_id=1, source_target_pairs={{0,16},{8,24},{16,0},{24,8},{1,17},{9,25},{17,1},{25,9},{2,18},{10... | collective-permute-start | bytes 294920 | tf_op jit(solution)/shard_map/ppermute | solution.py:397
  61.7 10.1 %collective-permute-start.2 = (f32[192,128]{1,0:T(8,128)S(1)}, f32[192,128]{1,0:T(8,128)S(1)}, u32[]{:S(2)}, u32[]{:S(2)}) collective-permute-start(f32[192,128]{1,0:T(8,128)S(1)} %collective-permute-done.refs_1_), channel_id=1, source_target_pairs={{0,16},{8,24},{16,0},{24,8},{1,17},{9,25},{17,1},{25,9},{2,18},{10... | collective-permute-start | bytes 294920 | tf_op jit(solution)/shard_map/ppermute | solution.py:397

commit v4 on v3

--- a/solution.py
+++ b/solution.py
@@ -9,7 +9,7 @@
 
 VBD = 64
 LANES = 128
-GROUP = 8
+GROUP = 16
 F32 = jnp.float32
 BF16 = jnp.bfloat16
 
@@ -390,12 +390,9 @@
         owner_last_kernel, "owner3", [VMEM] * 6, (f32(3 * VBD, LANES), f32(z.peers, LANES)),
         (VMEM,) * 2, exchange(msg), onehot, scal1, scal2, y1, y2,
     )
-    shares = [share]
-    hop = 1
-    while hop < n_ray:
-        pairs = [(r, r ^ hop) for r in range(n_ray)]
-        shares = shares + [lax.ppermute(s, "ray", pairs) for s in shares]
-        hop *= 2
+    shares = [share] + [
+        lax.ppermute(share, "ray", [(r, r ^ hop) for r in range(n_ray)]) for hop in range(1, n_ray)
+    ]
     return call(
         final_kernel, "final", [VMEM] * (1 + n_ray), (owned, owned), (VMEM,) * 2,
         exchange(back), *shares,

time: 72.7 us -> 72 us (level)
  blocking collectives: 61.5 us -> 59.7 us
  Pallas kernels: 7.44 us -> 8.71 us
    all_to_all x6, blocking collectives: 61.5 us -> 59.7 us  [exchange(): lax.all_to_all(x.reshape(n, 1, LANES), ('ray', 'vox'), 0, 0, tiled=True)]
    pallas_call x7, Pallas kernels: 7.44 us -> 8.71 us  [call(): pl.pallas_call(functools.partial(kernel, z), name=name, in_specs=in_specs...]
  transfers between devices with their start and end apart: 3 -> 3, of which waited for: 1 -> 0; matrix products, arithmetic and copies ran while one was open for 0% -> 0% of each run, Pallas kernels for 0% -> 0%
where the time goes in v4:
time: 72 us; the launch traced here: 71.7 us
  blocking collectives  59.7 us (83%)
  Pallas kernels  8.71 us (12%)
  starting transfers between devices  1.96 us (3%)
  between operations  1.32 us (2%)
    all_to_all x6, blocking collectives, exchange(): lax.all_to_all(x.reshape(n, 1, LANES), ('ray', 'vox'), 0, 0, tiled=True)  59.7 us
    pallas_call x7, Pallas kernels, call(): pl.pallas_call(functools.partial(kernel, z), name=name, in_specs=in_specs...  8.71 us
    ppermute x3, starting transfers between devices, on_device(): lax.ppermute(share, 'ray', [(r, r ^ hop) for r in range(n_ray)])  1.96 us
  transfers between devices with their start and end apart: 3, of which 0 were waited for; matrix products, arithmetic and copies ran while one was open for 0% of the time, Pallas kernels for 0%

profile of v4, /device:TPU:0, one launch (start us, length us, event | category | flops | bytes accessed | tf_op | source)
XLA Modules:
  0.0 71.7 jit_solution(16095762507253595613)
XLA Ops:
  1.3 2.7 %first.1 = (f32[160,128]{1,0:T(8,128)S(1)}, f32[16,128,128]{2,1,0:T(8,128)S(1)}, s32[65]{0:T(128)S(1)}, f32[64,128,128]{2,1,0:T(8,128)S(1)}) custom-call(s32[64]{0:T(128)} %ray_hbm.1, s32[64]{0:T(128)} %vox_hbm.1, s32[1]{0:T(128)S(6)} %copy.13.tile_count, f32[16,128]{1,0:T(8,128)} %travel_hbm.1, f32[64,128,128]{2,1,0:T(8,128)} %tiles_hbm.1), custom_call_target="tpu_custom_call" | custom-call | tf_op jit(solution)/shard_map/first/pallas_call | solution.py:341
  4.0 14.3 %all_to_all.30 = f32[160,1,128]{2,1,0:T(1,128)S(1)} all-to-all(f32[160,1,128]{2,1,0:T(1,128)S(1)} %bitcast.30), channel_id=1, replica_groups=mesh['ray'=4,'vox'=8] {'ray','vox'}, dimensions={0} | all-to-all | bytes 163840 | tf_op jit(solution)/shard_map/all_to_all | solution.py:348
  18.3 0.7 owner1.1
  19.0 9.1 %all_to_all.31 = f32[160,1,128]{2,1,0:T(1,128)S(1)} all-to-all(f32[160,1,128]{2,1,0:T(1,128)S(1)} %bitcast.31), channel_id=1, replica_groups=mesh['ray'=4,'vox'=8] {'ray','vox'}, dimensions={0} | all-to-all | bytes 163840 | tf_op jit(solution)/shard_map/all_to_all | solution.py:348
  28.1 1.8 %middle1.1 = (f32[160,128]{1,0:T(8,128)S(1)}, f32[8,128]{1,0:T(8,128)S(1)}, f32[16,128,128]{2,1,0:T(8,128)S(1)}) custom-call(s32[65]{0:T(128)S(1)} %get-tuple-element.19.code_v, f32[160,128]{1,0:T(8,128)S(1)} %bitcast.28, f32[16,128,128]{2,1,0:T(8,128)S(1)} %get-tuple-element.22.old, f32[64,128,128]{2,1,0:T(8,128)S(1)} %get-tuple-element.23.tiles_v), custom_call_target="tpu_custom_call" | custom-call | tf_op jit(solution)/shard_map/middle1/pallas_call | solution.py:341
  29.9 9.1 %all_to_all.32 = f32[160,1,128]{2,1,0:T(1,128)S(1)} all-to-all(f32[160,1,128]{2,1,0:T(1,128)S(1)} %bitcast.32), channel_id=1, replica_groups=mesh['ray'=4,'vox'=8] {'ray','vox'}, dimensions={0} | all-to-all | bytes 163840 | tf_op jit(solution)/shard_map/all_to_all | solution.py:348
  39.0 0.5 owner2.1
  39.6 9.1 %all_to_all.33 = f32[160,1,128]{2,1,0:T(1,128)S(1)} all-to-all(f32[160,1,128]{2,1,0:T(1,128)S(1)} %bitcast.33), channel_id=1, replica_groups=mesh['ray'=4,'vox'=8] {'ray','vox'}, dimensions={0} | all-to-all | bytes 163840 | tf_op jit(solution)/shard_map/all_to_all | solution.py:348
  48.7 1.9 %middle2.1 = (f32[160,128]{1,0:T(8,128)S(1)}, f32[8,128]{1,0:T(8,128)S(1)}) custom-call(s32[65]{0:T(128)S(1)} %get-tuple-element.19.code_v, f32[160,128]{1,0:T(8,128)S(1)} %bitcast.27, f32[16,128,128]{2,1,0:T(8,128)S(1)} %get-tuple-element.30.old, f32[64,128,128]{2,1,0:T(8,128)S(1)} %get-tuple-element.23.tiles_v), custom_call_target="tpu_custom_call" | custom-call | tf_op jit(solution)/shard_map/middle2/pallas_call | solution.py:341
  50.6 9.1 %all_to_all.34 = f32[160,1,128]{2,1,0:T(1,128)S(1)} all-to-all(f32[160,1,128]{2,1,0:T(1,128)S(1)} %bitcast.29), channel_id=1, replica_groups=mesh['ray'=4,'vox'=8] {'ray','vox'}, dimensions={0} | all-to-all | bytes 163840 | tf_op jit(solution)/shard_map/all_to_all | solution.py:348
  59.7 0.4 owner3.1
  60.2 0.3 collective-permute-start.2
  60.5 1.5 %collective-permute-start.1 = (f32[192,128]{1,0:T(8,128)S(1)}, f32[192,128]{1,0:T(8,128)S(1)}, u32[]{:S(2)}, u32[]{:S(2)}) collective-permute-start(f32[192,128]{1,0:T(8,128)S(1)} %get-tuple-element.35.refs_0_), channel_id=1, source_target_pairs={{0,16},{8,24},{16,0},{24,8},{1,17},{9,25},{17,1},{25,9},{2,18},{10... | collective-permute-start | bytes 294920 | tf_op jit(solution)/shard_map/ppermute | solution.py:394
  62.0 0.1 collective-permute-start
  62.1 8.8 %all_to_all.35 = f32[32,1,128]{2,1,0:T(1,128)S(1)} all-to-all(f32[32,1,128]{2,1,0:T(1,128)S(1)} %bitcast.35), channel_id=1, replica_groups=mesh['ray'=4,'vox'=8] {'ray','vox'}, dimensions={0} | all-to-all | bytes 32768 | tf_op jit(solution)/shard_map/all_to_all | solution.py:348
  70.9 0.0 collective-permute-done.2.refs_3_
  70.9 0.0 collective-permute-done.1.refs_2_
  70.9 0.0 collective-permute-done.refs_1_
  70.9 0.7 %final.1 = (f32[64,128]{1,0:T(8,128)}, f32[64,128]{1,0:T(8,128)}) custom-call(f32[32,128]{1,0:T(8,128)S(1)} %bitcast.34, f32[192,128]{1,0:T(8,128)S(1)} %get-tuple-element.35.refs_0_, f32[192,128]{1,0:T(8,128)S(1)} %collective-permute-done.refs_1_, f32[192,128]{1,0:T(8,128)S(1)} %collective-permute-done.1.refs_2_, f32[192,128]{1,0:T(8,128)S(1)} %collective-permute-done.2.refs_3_), custom_call_target="tpu_custom_call" | custom-call | tf_op jit(solution)/shard_map/final/pallas_call | solution.py:341
Async XLA Ops:
  60.2 10.8 %collective-permute-start.2 = (f32[192,128]{1,0:T(8,128)S(1)}, f32[192,128]{1,0:T(8,128)S(1)}, u32[]{:S(2)}, u32[]{:S(2)}) collective-permute-start(f32[192,128]{1,0:T(8,128)S(1)} %get-tuple-element.35.refs_0_), channel_id=1, source_target_pairs={{0,24},{8,16},{16,8},{24,0},{1,25},{9,17},{17,9},{25,1},{2,26},{10... | collective-permute-start | bytes 294920 | tf_op jit(solution)/shard_map/ppermute | solution.py:394
  60.5 10.4 %collective-permute-start.1 = (f32[192,128]{1,0:T(8,128)S(1)}, f32[192,128]{1,0:T(8,128)S(1)}, u32[]{:S(2)}, u32[]{:S(2)}) collective-permute-start(f32[192,128]{1,0:T(8,128)S(1)} %get-tuple-element.35.refs_0_), channel_id=1, source_target_pairs={{0,16},{8,24},{16,0},{24,8},{1,17},{9,25},{17,1},{25,9},{2,18},{10... | collective-permute-start | bytes 294920 | tf_op jit(solution)/shard_map/ppermute | solution.py:394
  62.0 9.0 %collective-permute-start = (f32[192,128]{1,0:T(8,128)S(1)}, f32[192,128]{1,0:T(8,128)S(1)}, u32[]{:S(2)}, u32[]{:S(2)}) collective-permute-start(f32[192,128]{1,0:T(8,128)S(1)} %get-tuple-element.35.refs_0_), channel_id=1, source_target_pairs={{0,8},{8,0},{16,24},{24,16},{1,9},{9,1},{17,25},{25,17},{2,10},{10... | collective-permute-start | bytes 294920 | tf_op jit(solution)/shard_map/ppermute | solution.py:394

commit v5 on v4

--- a/solution.py
+++ b/solution.py
@@ -93,8 +93,8 @@
 
 
 def first_kernel(
-    z, ray_hbm, vox_hbm, tile_count, travel_hbm, tiles_hbm, msg, wide, code_out, tiles_v,
-    prod, named, pad, tile_ray, tile_vox, travel, code, count, sem, small_sem, code_sem,
+    z, ray_hbm, vox_hbm, tile_count, travel_hbm, tiles_hbm, msg, wide, code, tiles_v,
+    prod, named, pad, tile_ray, tile_vox, travel, count, sem, small_sem,
 ):
     small = [
         pltpu.make_async_copy(src, dst, small_sem.at[i])
@@ -116,6 +116,7 @@
         count[o] = 0
     prod[...] = jnp.zeros_like(prod)
     named[...] = jnp.full_like(named, -1.0)
+    code[...] = jnp.zeros_like(code)
     pad[...] = jnp.zeros_like(pad)
     small[0].wait()
     pad[pl.ds(0, z.ray_blocks), :] = travel[...]
@@ -134,29 +135,26 @@
         k = count[owner]
         count[owner] = k + 1
         row = k * z.n_vox + owner
-        code[t] = row * 256 + ray
+        code[pl.ds(t, 1), :] = jnp.full((1, LANES), row * 256 + ray, jnp.int32)
         block = jnp.where(t < live, vox & (VBD - 1), -1).astype(F32)
         named[pl.ds(row, 1), :] = jnp.full((1, LANES), block, F32)
         return ray, row
 
-    code[z.slots] = groups
+    code[pl.ds(z.slots, 1), :] = jnp.full((1, LANES), groups, jnp.int32)
     backward(groups, where_of, tiles_v, wide, prod, ready)
-    keep = pltpu.make_async_copy(code, code_out, code_sem)
-    keep.start()
     here = lane((z.n_vox, LANES))
     meta = jnp.where(here == z.cap, total(travel[...] * travel[...]), 0.0)
     for k in range(z.cap):
         meta = jnp.where(here == k, named[pl.ds(k * z.n_vox, z.n_vox), :], meta)
     write_products(z, prod, msg, meta)
-    keep.wait()
 
 
 def middle_kernel(
     z, code_v, back, old, tiles_v, msg, scal, *refs
 ):
-    wide, prod, vox_rows, sums, sems, code, code_sem = refs
-    fetch = pltpu.make_async_copy(code_v, code, code_sem)
-    fetch.start()
+    wide, prod, vox_rows, sums, sems, code = refs
+    for t in range(z.slots + 1):
+        code[t] = code_v[t, 0]
     meta = back[pl.ds(z.data_rows, z.peers, stride=z.rows), :]
     alpha = jnp.sqrt(pick(jnp.sum(meta, axis=0, keepdims=True), 0))
     beta = pick(meta[0:1], 1)
@@ -178,7 +176,6 @@
         sums[r] = old[r] * lane_share
         sems[r] = jnp.zeros((LANES, LANES), F32)
     prod[...] = jnp.zeros_like(prod)
-    fetch.wait()
     groups = code[z.slots]
 
     def where_of(t):
@@ -351,11 +348,11 @@
     per_ray = pltpu.VMEM((z.ray_blocks, LANES, LANES), F32)
     compact = pltpu.VMEM((z.compact, LANES), F32)
     indices = pltpu.SMEM((z.slots,), jnp.int32)
+
     codes = pltpu.SMEM((z.slots + 1,), jnp.int32)
-    one_sem = pltpu.SemaphoreType.DMA(())
 
     def middle(back, wide, last):
-        scratch = (compact, compact, per_ray, per_ray, codes, one_sem)
+        scratch = (compact, compact, per_ray, per_ray, codes)
         out = (message, f32(8, LANES))
         return call(
             middle_kernel, "middle2" if last else "middle1", (VMEM,) * 4,
@@ -365,13 +362,13 @@
 
     msg, wide, code, tiles_v = call(
         first_kernel, "first", [HBM, HBM, SMEM, HBM, HBM],
-        (message, wide_rays, jax.ShapeDtypeStruct((z.slots + 1,), jnp.int32), f32(*tiles.shape)),
+        (message, wide_rays, jax.ShapeDtypeStruct((z.slots + 8, LANES), jnp.int32), f32(*tiles.shape)),
         (VMEM,) * 4,
         in_hbm(tile_ray), in_hbm(tile_vox), tile_count, in_hbm(travel), in_hbm(tiles),
         scratch=(
             compact, compact, pltpu.VMEM((LANES, LANES), F32), indices, indices,
-            pltpu.VMEM(travel.shape, F32), codes, pltpu.SMEM((z.n_vox,), jnp.int32),
-            pltpu.SemaphoreType.DMA((z.slots // GROUP,)), pltpu.SemaphoreType.DMA((3,)), one_sem,
+            pltpu.VMEM(travel.shape, F32), pltpu.SMEM((z.n_vox,), jnp.int32),
+            pltpu.SemaphoreType.DMA((z.slots // GROUP,)), pltpu.SemaphoreType.DMA((3,)),
         ),
     )
     n, m = z.data_rows * z.peers, z.segs * VBD

time: 72 us -> 70.3 us (0.976)
  Pallas kernels: 8.71 us -> 7.52 us
    pallas_call x7, Pallas kernels: 8.71 us -> 7.52 us  [call(): pl.pallas_call(functools.partial(kernel, z), name=name, in_specs=in_specs...]
where the time goes in v5:
time: 70.3 us
  blocking collectives  59.5 us (85%)
  Pallas kernels  7.52 us (11%)
  starting transfers between devices  1.96 us (3%)
  between operations  1.32 us (2%)
    all_to_all x6, blocking collectives, exchange(): lax.all_to_all(x.reshape(n, 1, LANES), ('ray', 'vox'), 0, 0, tiled=True)  59.5 us
    pallas_call x7, Pallas kernels, call(): pl.pallas_call(functools.partial(kernel, z), name=name, in_specs=in_specs...  7.52 us
    ppermute x3, starting transfers between devices, on_device(): lax.ppermute(share, 'ray', [(r, r ^ hop) for r in range(n_ray)])  1.96 us
  transfers between devices with their start and end apart: 3, of which 0 were waited for; matrix products, arithmetic and copies ran while one was open for 0% of the time, Pallas kernels for 0%

profile of v5, /device:TPU:0, one launch (start us, length us, event | category | flops | bytes accessed | tf_op | source)
XLA Modules:
  0.0 70.3 jit_solution(5971133106005442379)
XLA Ops:
  1.3 2.2 %first.1 = (f32[160,128]{1,0:T(8,128)S(1)}, f32[16,128,128]{2,1,0:T(8,128)S(1)}, s32[72,128]{1,0:T(8,128)S(1)}, f32[64,128,128]{2,1,0:T(8,128)S(1)}) custom-call(s32[64]{0:T(128)} %ray_hbm.1, s32[64]{0:T(128)} %vox_hbm.1, s32[1]{0:T(128)S(6)} %copy.13.tile_count, f32[16,128]{1,0:T(8,128)} %travel_hbm.1, f32[64,128,128]{2,1,0:T(8,128)} %tiles_hbm.1), custom_call_target="tpu_custom_call" | custom-call | tf_op jit(solution)/shard_map/first/pallas_call | solution.py:338
  3.5 14.2 %all_to_all.30 = f32[160,1,128]{2,1,0:T(1,128)S(1)} all-to-all(f32[160,1,128]{2,1,0:T(1,128)S(1)} %bitcast.30), channel_id=1, replica_groups=mesh['ray'=4,'vox'=8] {'ray','vox'}, dimensions={0} | all-to-all | bytes 163840 | tf_op jit(solution)/shard_map/all_to_all | solution.py:345
  17.7 0.7 %owner1.1 = (f32[160,128]{1,0:T(8,128)S(1)}, f32[64,128]{1,0:T(8,128)S(1)}, bf16[256,128]{1,0:T(8,128)(2,1)S(1)}, bf16[128,256]{1,0:T(8,128)(2,1)S(1)}) custom-call(f32[160,128]{1,0:T(8,128)S(1)} %bitcast.25), custom_call_target="tpu_custom_call" | custom-call | tf_op jit(solution)/shard_map/owner1/pallas_call | solution.py:338
  18.4 9.1 %all_to_all.31 = f32[160,1,128]{2,1,0:T(1,128)S(1)} all-to-all(f32[160,1,128]{2,1,0:T(1,128)S(1)} %bitcast.31), channel_id=1, replica_groups=mesh['ray'=4,'vox'=8] {'ray','vox'}, dimensions={0} | all-to-all | bytes 163840 | tf_op jit(solution)/shard_map/all_to_all | solution.py:345
  27.5 1.4 %middle1.1 = (f32[160,128]{1,0:T(8,128)S(1)}, f32[8,128]{1,0:T(8,128)S(1)}, f32[16,128,128]{2,1,0:T(8,128)S(1)}) custom-call(s32[72,128]{1,0:T(8,128)S(1)} %get-tuple-element.19.code_v, f32[160,128]{1,0:T(8,128)S(1)} %bitcast.28, f32[16,128,128]{2,1,0:T(8,128)S(1)} %get-tuple-element.22.old, f32[64,128,128]{2,1,0:T(8,128)S(1)} %get-tuple-element.23.tiles_v), custom_call_target="tpu_custom_call" | custom-call | tf_op jit(solution)/shard_map/middle1/pallas_call | solution.py:338
  28.9 9.1 %all_to_all.32 = f32[160,1,128]{2,1,0:T(1,128)S(1)} all-to-all(f32[160,1,128]{2,1,0:T(1,128)S(1)} %bitcast.32), channel_id=1, replica_groups=mesh['ray'=4,'vox'=8] {'ray','vox'}, dimensions={0} | all-to-all | bytes 163840 | tf_op jit(solution)/shard_map/all_to_all | solution.py:345
  38.1 0.5 owner2.1
  38.6 9.1 %all_to_all.33 = f32[160,1,128]{2,1,0:T(1,128)S(1)} all-to-all(f32[160,1,128]{2,1,0:T(1,128)S(1)} %bitcast.33), channel_id=1, replica_groups=mesh['ray'=4,'vox'=8] {'ray','vox'}, dimensions={0} | all-to-all | bytes 163840 | tf_op jit(solution)/shard_map/all_to_all | solution.py:345
  47.7 1.5 %middle2.1 = (f32[160,128]{1,0:T(8,128)S(1)}, f32[8,128]{1,0:T(8,128)S(1)}) custom-call(s32[72,128]{1,0:T(8,128)S(1)} %get-tuple-element.19.code_v, f32[160,128]{1,0:T(8,128)S(1)} %bitcast.27, f32[16,128,128]{2,1,0:T(8,128)S(1)} %get-tuple-element.30.old, f32[64,128,128]{2,1,0:T(8,128)S(1)} %get-tuple-element.23.tiles_v), custom_call_target="tpu_custom_call" | custom-call | tf_op jit(solution)/shard_map/middle2/pallas_call | solution.py:338
  49.2 9.1 %all_to_all.34 = f32[160,1,128]{2,1,0:T(1,128)S(1)} all-to-all(f32[160,1,128]{2,1,0:T(1,128)S(1)} %bitcast.29), channel_id=1, replica_groups=mesh['ray'=4,'vox'=8] {'ray','vox'}, dimensions={0} | all-to-all | bytes 163840 | tf_op jit(solution)/shard_map/all_to_all | solution.py:345
  58.4 0.4 owner3.1
  58.8 0.3 collective-permute-start.2
  59.2 1.5 %collective-permute-start.1 = (f32[192,128]{1,0:T(8,128)S(1)}, f32[192,128]{1,0:T(8,128)S(1)}, u32[]{:S(2)}, u32[]{:S(2)}) collective-permute-start(f32[192,128]{1,0:T(8,128)S(1)} %get-tuple-element.35.refs_0_), channel_id=1, source_target_pairs={{0,16},{8,24},{16,0},{24,8},{1,17},{9,25},{17,1},{25,9},{2,18},{10... | collective-permute-start | bytes 294920 | tf_op jit(solution)/shard_map/ppermute | solution.py:391
  60.6 0.1 collective-permute-start
  60.8 8.8 %all_to_all.35 = f32[32,1,128]{2,1,0:T(1,128)S(1)} all-to-all(f32[32,1,128]{2,1,0:T(1,128)S(1)} %bitcast.35), channel_id=1, replica_groups=mesh['ray'=4,'vox'=8] {'ray','vox'}, dimensions={0} | all-to-all | bytes 32768 | tf_op jit(solution)/shard_map/all_to_all | solution.py:345
  69.6 0.0 collective-permute-done.2.refs_3_
  69.6 0.0 collective-permute-done.1.refs_2_
  69.6 0.0 collective-permute-done.refs_1_
  69.6 0.7 %final.1 = (f32[64,128]{1,0:T(8,128)}, f32[64,128]{1,0:T(8,128)}) custom-call(f32[32,128]{1,0:T(8,128)S(1)} %bitcast.34, f32[192,128]{1,0:T(8,128)S(1)} %get-tuple-element.35.refs_0_, f32[192,128]{1,0:T(8,128)S(1)} %collective-permute-done.refs_1_, f32[192,128]{1,0:T(8,128)S(1)} %collective-permute-done.1.refs_2_, f32[192,128]{1,0:T(8,128)S(1)} %collective-permute-done.2.refs_3_), custom_call_target="tpu_custom_call" | custom-call | tf_op jit(solution)/shard_map/final/pallas_call | solution.py:338
Async XLA Ops:
  58.8 10.8 %collective-permute-start.2 = (f32[192,128]{1,0:T(8,128)S(1)}, f32[192,128]{1,0:T(8,128)S(1)}, u32[]{:S(2)}, u32[]{:S(2)}) collective-permute-start(f32[192,128]{1,0:T(8,128)S(1)} %get-tuple-element.35.refs_0_), channel_id=1, source_target_pairs={{0,24},{8,16},{16,8},{24,0},{1,25},{9,17},{17,9},{25,1},{2,26},{10... | collective-permute-start | bytes 294920 | tf_op jit(solution)/shard_map/ppermute | solution.py:391
  59.2 10.4 %collective-permute-start.1 = (f32[192,128]{1,0:T(8,128)S(1)}, f32[192,128]{1,0:T(8,128)S(1)}, u32[]{:S(2)}, u32[]{:S(2)}) collective-permute-start(f32[192,128]{1,0:T(8,128)S(1)} %get-tuple-element.35.refs_0_), channel_id=1, source_target_pairs={{0,16},{8,24},{16,0},{24,8},{1,17},{9,25},{17,1},{25,9},{2,18},{10... | collective-permute-start | bytes 294920 | tf_op jit(solution)/shard_map/ppermute | solution.py:391
  60.6 9.0 %collective-permute-start = (f32[192,128]{1,0:T(8,128)S(1)}, f32[192,128]{1,0:T(8,128)S(1)}, u32[]{:S(2)}, u32[]{:S(2)}) collective-permute-start(f32[192,128]{1,0:T(8,128)S(1)} %get-tuple-element.35.refs_0_), channel_id=1, source_target_pairs={{0,8},{8,0},{16,24},{24,16},{1,9},{9,1},{17,25},{25,17},{2,10},{10... | collective-permute-start | bytes 294920 | tf_op jit(solution)/shard_map/ppermute | solution.py:391

commit v6 on v5

--- a/solution.py
+++ b/solution.py
@@ -121,8 +121,20 @@
     small[0].wait()
     pad[pl.ds(0, z.ray_blocks), :] = travel[...]
     by_col = pad[...].T
+    parts = split3(by_col)
+    packed = parts[:, :LANES].astype(F32)
+    for i in (1, 2):
+        packed += shift_lanes(parts[:, i * LANES : (i + 1) * LANES].astype(F32), i * z.ray_blocks)
+    packed = packed.astype(BF16)
+    from_row = lax.broadcasted_iota(jnp.int32, (LANES, LANES), 0)
+    from_row = jnp.where(from_row < 3 * z.ray_blocks, from_row % z.ray_blocks, -1)
+    ones = jnp.ones((LANES, LANES), F32)
     for r in range(z.ray_blocks):
-        wide[r] = jnp.broadcast_to(by_col[:, r : r + 1], (LANES, LANES))
+        if r % 2:
+            from_lane = jnp.where(from_row == r, ones, 0.0).astype(BF16)
+            wide[r] = jnp.dot(packed, from_lane, preferred_element_type=F32)
+        else:
+            wide[r] = jnp.broadcast_to(by_col[:, r : r + 1], (LANES, LANES))
     for copy in small[1:]:
         copy.wait()
 
@@ -193,9 +205,12 @@
     lax.fori_loop(0, groups, step, 0)
     square = jnp.zeros((LANES, LANES), F32)
     for r in range(z.ray_blocks):
-        u = jnp.broadcast_to(
-            jnp.sum(sums[r] + sems[r], axis=1, keepdims=True), (LANES, LANES)
-        )
+        both = sums[r] + sems[r]
+        if r % 4 == 3:
+            ones = jnp.ones((3 * LANES, LANES), BF16)
+            u = jnp.dot(split3(both), ones, preferred_element_type=F32)
+        else:
+            u = jnp.broadcast_to(jnp.sum(both, axis=1, keepdims=True), (LANES, LANES))
         wide[r] = u
         square += u * u
     backward(groups, where_of, tiles_v, wide, prod)

time: 70.3 us -> 70.8 us (level)
  no operation moved by 1% of the time
where the time goes in v6:
time: 70.8 us; the launch traced here: 71 us
  blocking collectives  60.2 us (85%)
  Pallas kernels  7.48 us (11%)
  starting transfers between devices  1.96 us (3%)
  between operations  1.32 us (2%)
    all_to_all x6, blocking collectives, exchange(): lax.all_to_all(x.reshape(n, 1, LANES), ('ray', 'vox'), 0, 0, tiled=True)  60.2 us
    pallas_call x7, Pallas kernels, call(): pl.pallas_call(functools.partial(kernel, z), name=name, in_specs=in_specs...  7.48 us
    ppermute x3, starting transfers between devices, on_device(): lax.ppermute(share, 'ray', [(r, r ^ hop) for r in range(n_ray)])  1.96 us
  transfers between devices with their start and end apart: 3, of which 0 were waited for; matrix products, arithmetic and copies ran while one was open for 0% of the time, Pallas kernels for 0%

profile of v6, /device:TPU:0, one launch (start us, length us, event | category | flops | bytes accessed | tf_op | source)
XLA Modules:
  0.0 71.0 jit_solution(3442262073175589999)
XLA Ops:
  1.3 2.2 %first.1 = (f32[160,128]{1,0:T(8,128)S(1)}, f32[16,128,128]{2,1,0:T(8,128)S(1)}, s32[72,128]{1,0:T(8,128)S(1)}, f32[64,128,128]{2,1,0:T(8,128)S(1)}) custom-call(s32[64]{0:T(128)} %ray_hbm.1, s32[64]{0:T(128)} %vox_hbm.1, s32[1]{0:T(128)S(6)} %copy.13.tile_count, f32[16,128]{1,0:T(8,128)} %travel_hbm.1, f32[64,128,128]{2,1,0:T(8,128)} %tiles_hbm.1), custom_call_target="tpu_custom_call" | custom-call | tf_op jit(solution)/shard_map/first/pallas_call | solution.py:353
  3.5 14.9 %all_to_all.30 = f32[160,1,128]{2,1,0:T(1,128)S(1)} all-to-all(f32[160,1,128]{2,1,0:T(1,128)S(1)} %bitcast.30), channel_id=1, replica_groups=mesh['ray'=4,'vox'=8] {'ray','vox'}, dimensions={0} | all-to-all | bytes 163840 | tf_op jit(solution)/shard_map/all_to_all | solution.py:360
  18.4 0.7 %owner1.1 = (f32[160,128]{1,0:T(8,128)S(1)}, f32[64,128]{1,0:T(8,128)S(1)}, bf16[256,128]{1,0:T(8,128)(2,1)S(1)}, bf16[128,256]{1,0:T(8,128)(2,1)S(1)}) custom-call(f32[160,128]{1,0:T(8,128)S(1)} %bitcast.25), custom_call_target="tpu_custom_call" | custom-call | tf_op jit(solution)/shard_map/owner1/pallas_call | solution.py:353
  19.1 9.1 %all_to_all.31 = f32[160,1,128]{2,1,0:T(1,128)S(1)} all-to-all(f32[160,1,128]{2,1,0:T(1,128)S(1)} %bitcast.31), channel_id=1, replica_groups=mesh['ray'=4,'vox'=8] {'ray','vox'}, dimensions={0} | all-to-all | bytes 163840 | tf_op jit(solution)/shard_map/all_to_all | solution.py:360
  28.2 1.3 %middle1.1 = (f32[160,128]{1,0:T(8,128)S(1)}, f32[8,128]{1,0:T(8,128)S(1)}, f32[16,128,128]{2,1,0:T(8,128)S(1)}) custom-call(s32[72,128]{1,0:T(8,128)S(1)} %get-tuple-element.19.code_v, f32[160,128]{1,0:T(8,128)S(1)} %bitcast.28, f32[16,128,128]{2,1,0:T(8,128)S(1)} %get-tuple-element.22.old, f32[64,128,128]{2,1,0:T(8,128)S(1)} %get-tuple-element.23.tiles_v), custom_call_target="tpu_custom_call" | custom-call | tf_op jit(solution)/shard_map/middle1/pallas_call | solution.py:353
  29.6 9.1 %all_to_all.32 = f32[160,1,128]{2,1,0:T(1,128)S(1)} all-to-all(f32[160,1,128]{2,1,0:T(1,128)S(1)} %bitcast.32), channel_id=1, replica_groups=mesh['ray'=4,'vox'=8] {'ray','vox'}, dimensions={0} | all-to-all | bytes 163840 | tf_op jit(solution)/shard_map/all_to_all | solution.py:360
  38.7 0.5 owner2.1
  39.3 9.1 %all_to_all.33 = f32[160,1,128]{2,1,0:T(1,128)S(1)} all-to-all(f32[160,1,128]{2,1,0:T(1,128)S(1)} %bitcast.33), channel_id=1, replica_groups=mesh['ray'=4,'vox'=8] {'ray','vox'}, dimensions={0} | all-to-all | bytes 163840 | tf_op jit(solution)/shard_map/all_to_all | solution.py:360
  48.4 1.5 %middle2.1 = (f32[160,128]{1,0:T(8,128)S(1)}, f32[8,128]{1,0:T(8,128)S(1)}) custom-call(s32[72,128]{1,0:T(8,128)S(1)} %get-tuple-element.19.code_v, f32[160,128]{1,0:T(8,128)S(1)} %bitcast.27, f32[16,128,128]{2,1,0:T(8,128)S(1)} %get-tuple-element.30.old, f32[64,128,128]{2,1,0:T(8,128)S(1)} %get-tuple-element.23.tiles_v), custom_call_target="tpu_custom_call" | custom-call | tf_op jit(solution)/shard_map/middle2/pallas_call | solution.py:353
  49.9 9.1 %all_to_all.34 = f32[160,1,128]{2,1,0:T(1,128)S(1)} all-to-all(f32[160,1,128]{2,1,0:T(1,128)S(1)} %bitcast.29), channel_id=1, replica_groups=mesh['ray'=4,'vox'=8] {'ray','vox'}, dimensions={0} | all-to-all | bytes 163840 | tf_op jit(solution)/shard_map/all_to_all | solution.py:360
  59.0 0.4 owner3.1
  59.5 0.3 collective-permute-start.2
  59.8 1.5 %collective-permute-start.1 = (f32[192,128]{1,0:T(8,128)S(1)}, f32[192,128]{1,0:T(8,128)S(1)}, u32[]{:S(2)}, u32[]{:S(2)}) collective-permute-start(f32[192,128]{1,0:T(8,128)S(1)} %get-tuple-element.35.refs_0_), channel_id=1, source_target_pairs={{0,16},{8,24},{16,0},{24,8},{1,17},{9,25},{17,1},{25,9},{2,18},{10... | collective-permute-start | bytes 294920 | tf_op jit(solution)/shard_map/ppermute | solution.py:406
  61.3 0.1 collective-permute-start
  61.4 8.8 %all_to_all.35 = f32[32,1,128]{2,1,0:T(1,128)S(1)} all-to-all(f32[32,1,128]{2,1,0:T(1,128)S(1)} %bitcast.35), channel_id=1, replica_groups=mesh['ray'=4,'vox'=8] {'ray','vox'}, dimensions={0} | all-to-all | bytes 32768 | tf_op jit(solution)/shard_map/all_to_all | solution.py:360
  70.2 0.0 collective-permute-done.2.refs_3_
  70.2 0.0 collective-permute-done.1.refs_2_
  70.2 0.0 collective-permute-done.refs_1_
  70.2 0.7 %final.1 = (f32[64,128]{1,0:T(8,128)}, f32[64,128]{1,0:T(8,128)}) custom-call(f32[32,128]{1,0:T(8,128)S(1)} %bitcast.34, f32[192,128]{1,0:T(8,128)S(1)} %get-tuple-element.35.refs_0_, f32[192,128]{1,0:T(8,128)S(1)} %collective-permute-done.refs_1_, f32[192,128]{1,0:T(8,128)S(1)} %collective-permute-done.1.refs_2_, f32[192,128]{1,0:T(8,128)S(1)} %collective-permute-done.2.refs_3_), custom_call_target="tpu_custom_call" | custom-call | tf_op jit(solution)/shard_map/final/pallas_call | solution.py:353
Async XLA Ops:
  59.5 10.8 %collective-permute-start.2 = (f32[192,128]{1,0:T(8,128)S(1)}, f32[192,128]{1,0:T(8,128)S(1)}, u32[]{:S(2)}, u32[]{:S(2)}) collective-permute-start(f32[192,128]{1,0:T(8,128)S(1)} %get-tuple-element.35.refs_0_), channel_id=1, source_target_pairs={{0,24},{8,16},{16,8},{24,0},{1,25},{9,17},{17,9},{25,1},{2,26},{10... | collective-permute-start | bytes 294920 | tf_op jit(solution)/shard_map/ppermute | solution.py:406
  59.8 10.4 %collective-permute-start.1 = (f32[192,128]{1,0:T(8,128)S(1)}, f32[192,128]{1,0:T(8,128)S(1)}, u32[]{:S(2)}, u32[]{:S(2)}) collective-permute-start(f32[192,128]{1,0:T(8,128)S(1)} %get-tuple-element.35.refs_0_), channel_id=1, source_target_pairs={{0,16},{8,24},{16,0},{24,8},{1,17},{9,25},{17,1},{25,9},{2,18},{10... | collective-permute-start | bytes 294920 | tf_op jit(solution)/shard_map/ppermute | solution.py:406
  61.3 9.0 %collective-permute-start = (f32[192,128]{1,0:T(8,128)S(1)}, f32[192,128]{1,0:T(8,128)S(1)}, u32[]{:S(2)}, u32[]{:S(2)}) collective-permute-start(f32[192,128]{1,0:T(8,128)S(1)} %get-tuple-element.35.refs_0_), channel_id=1, source_target_pairs={{0,8},{8,0},{16,24},{24,16},{1,9},{9,1},{17,25},{25,17},{2,10},{10... | collective-permute-start | bytes 294920 | tf_op jit(solution)/shard_map/ppermute | solution.py:406

commit v7 on v5

--- a/solution.py
+++ b/solution.py
@@ -152,7 +152,8 @@
 def middle_kernel(
     z, code_v, back, old, tiles_v, msg, scal, *refs
 ):
-    wide, prod, vox_rows, sums, sems, code = refs
+    prod, vox_rows, sums, sems, code = refs[-5:]
+    wide = refs[0] if len(refs) > 5 else sums
     for t in range(z.slots + 1):
         code[t] = code_v[t, 0]
     meta = back[pl.ds(z.data_rows, z.peers, stride=z.rows), :]
@@ -193,9 +194,12 @@
     lax.fori_loop(0, groups, step, 0)
     square = jnp.zeros((LANES, LANES), F32)
     for r in range(z.ray_blocks):
-        u = jnp.broadcast_to(
-            jnp.sum(sums[r] + sems[r], axis=1, keepdims=True), (LANES, LANES)
-        )
+        both = sums[r] + sems[r]
+        if r % 4 == 3:
+            ones = jnp.ones((3 * LANES, LANES), BF16)
+            u = jnp.dot(split3(both), ones, preferred_element_type=F32)
+        else:
+            u = jnp.broadcast_to(jnp.sum(both, axis=1, keepdims=True), (LANES, LANES))
         wide[r] = u
         square += u * u
     backward(groups, where_of, tiles_v, wide, prod)
@@ -357,7 +361,7 @@
         return call(
             middle_kernel, "middle2" if last else "middle1", (VMEM,) * 4,
             out if last else out + (wide_rays,), (VMEM,) * (2 if last else 3),
-            code, back, wide, tiles_v, scratch=(per_ray,) + scratch if last else scratch,
+            code, back, wide, tiles_v, scratch=scratch,
         )
 
     msg, wide, code, tiles_v = call(

time: 70.3 us -> 70.6 us (level)
  blocking collectives: 59.5 us -> 61.3 us
  Pallas kernels: 7.52 us -> 6.08 us
    all_to_all x6, blocking collectives: 59.5 us -> 61.3 us  [exchange(): lax.all_to_all(x.reshape(n, 1, LANES), ('ray', 'vox'), 0, 0, tiled=True)]
    pallas_call x7, Pallas kernels: 7.52 us -> 6.08 us  [call(): pl.pallas_call(functools.partial(kernel, z), name=name, in_specs=in_specs...]
where the time goes in v7:
time: 70.6 us
  blocking collectives  61.3 us (87%)
  Pallas kernels  6.08 us (9%)
  starting transfers between devices  1.96 us (3%)
  between operations  1.32 us (2%)
    all_to_all x6, blocking collectives, exchange(): lax.all_to_all(x.reshape(n, 1, LANES), ('ray', 'vox'), 0, 0, tiled=True)  61.3 us
    pallas_call x7, Pallas kernels, call(): pl.pallas_call(functools.partial(kernel, z), name=name, in_specs=in_specs...  6.08 us
    ppermute x3, starting transfers between devices, on_device(): lax.ppermute(share, 'ray', [(r, r ^ hop) for r in range(n_ray)])  1.96 us
  transfers between devices with their start and end apart: 3, of which 0 were waited for; matrix products, arithmetic and copies ran while one was open for 0% of the time, Pallas kernels for 0%

profile of v7, /device:TPU:0, one launch (start us, length us, event | category | flops | bytes accessed | tf_op | source)
XLA Modules:
  0.0 70.6 jit_solution(15157650074033046437)
XLA Ops:
  1.3 1.9 %first.1 = (f32[160,128]{1,0:T(8,128)S(1)}, f32[16,128,128]{2,1,0:T(8,128)S(1)}, s32[72,128]{1,0:T(8,128)S(1)}, f32[64,128,128]{2,1,0:T(8,128)S(1)}) custom-call(s32[64]{0:T(128)} %ray_hbm.1, s32[64]{0:T(128)} %vox_hbm.1, s32[1]{0:T(128)S(6)} %copy.13.tile_count, f32[16,128]{1,0:T(8,128)} %travel_hbm.1, f32[64,128,128]{2,1,0:T(8,128)} %tiles_hbm.1), custom_call_target="tpu_custom_call" | custom-call | tf_op jit(solution)/shard_map/first/pallas_call | solution.py:342
  3.2 15.2 %all_to_all.30 = f32[160,1,128]{2,1,0:T(1,128)S(1)} all-to-all(f32[160,1,128]{2,1,0:T(1,128)S(1)} %bitcast.30), channel_id=1, replica_groups=mesh['ray'=4,'vox'=8] {'ray','vox'}, dimensions={0} | all-to-all | bytes 163840 | tf_op jit(solution)/shard_map/all_to_all | solution.py:349
  18.4 0.7 %owner1.1 = (f32[160,128]{1,0:T(8,128)S(1)}, f32[64,128]{1,0:T(8,128)S(1)}, bf16[256,128]{1,0:T(8,128)(2,1)S(1)}, bf16[128,256]{1,0:T(8,128)(2,1)S(1)}) custom-call(f32[160,128]{1,0:T(8,128)S(1)} %bitcast.25), custom_call_target="tpu_custom_call" | custom-call | tf_op jit(solution)/shard_map/owner1/pallas_call | solution.py:342
  19.1 9.1 %all_to_all.31 = f32[160,1,128]{2,1,0:T(1,128)S(1)} all-to-all(f32[160,1,128]{2,1,0:T(1,128)S(1)} %bitcast.31), channel_id=1, replica_groups=mesh['ray'=4,'vox'=8] {'ray','vox'}, dimensions={0} | all-to-all | bytes 163840 | tf_op jit(solution)/shard_map/all_to_all | solution.py:349
  28.2 0.9 %middle1.1 = (f32[160,128]{1,0:T(8,128)S(1)}, f32[8,128]{1,0:T(8,128)S(1)}, f32[16,128,128]{2,1,0:T(8,128)S(1)}) custom-call(s32[72,128]{1,0:T(8,128)S(1)} %get-tuple-element.19.code_v, f32[160,128]{1,0:T(8,128)S(1)} %bitcast.28, f32[16,128,128]{2,1,0:T(8,128)S(1)} %get-tuple-element.22.old, f32[64,128,128]{2,1,0:T(8,128)S(1)} %get-tuple-element.23.tiles_v), custom_call_target="tpu_custom_call" | custom-call | tf_op jit(solution)/shard_map/middle1/pallas_call | solution.py:342
  29.1 9.4 %all_to_all.32 = f32[160,1,128]{2,1,0:T(1,128)S(1)} all-to-all(f32[160,1,128]{2,1,0:T(1,128)S(1)} %bitcast.32), channel_id=1, replica_groups=mesh['ray'=4,'vox'=8] {'ray','vox'}, dimensions={0} | all-to-all | bytes 163840 | tf_op jit(solution)/shard_map/all_to_all | solution.py:349
  38.5 0.5 owner2.1
  39.1 9.1 %all_to_all.33 = f32[160,1,128]{2,1,0:T(1,128)S(1)} all-to-all(f32[160,1,128]{2,1,0:T(1,128)S(1)} %bitcast.33), channel_id=1, replica_groups=mesh['ray'=4,'vox'=8] {'ray','vox'}, dimensions={0} | all-to-all | bytes 163840 | tf_op jit(solution)/shard_map/all_to_all | solution.py:349
  48.2 0.9 %middle2.1 = (f32[160,128]{1,0:T(8,128)S(1)}, f32[8,128]{1,0:T(8,128)S(1)}) custom-call(s32[72,128]{1,0:T(8,128)S(1)} %get-tuple-element.19.code_v, f32[160,128]{1,0:T(8,128)S(1)} %bitcast.27, f32[16,128,128]{2,1,0:T(8,128)S(1)} %get-tuple-element.30.old, f32[64,128,128]{2,1,0:T(8,128)S(1)} %get-tuple-element.23.tiles_v), custom_call_target="tpu_custom_call" | custom-call | tf_op jit(solution)/shard_map/middle2/pallas_call | solution.py:342
  49.1 9.6 %all_to_all.34 = f32[160,1,128]{2,1,0:T(1,128)S(1)} all-to-all(f32[160,1,128]{2,1,0:T(1,128)S(1)} %bitcast.29), channel_id=1, replica_groups=mesh['ray'=4,'vox'=8] {'ray','vox'}, dimensions={0} | all-to-all | bytes 163840 | tf_op jit(solution)/shard_map/all_to_all | solution.py:349
  58.7 0.4 owner3.1
  59.1 0.3 collective-permute-start.2
  59.5 1.5 %collective-permute-start.1 = (f32[192,128]{1,0:T(8,128)S(1)}, f32[192,128]{1,0:T(8,128)S(1)}, u32[]{:S(2)}, u32[]{:S(2)}) collective-permute-start(f32[192,128]{1,0:T(8,128)S(1)} %get-tuple-element.35.refs_0_), channel_id=1, source_target_pairs={{0,16},{8,24},{16,0},{24,8},{1,17},{9,25},{17,1},{25,9},{2,18},{10... | collective-permute-start | bytes 294920 | tf_op jit(solution)/shard_map/ppermute | solution.py:395
  60.9 0.1 collective-permute-start
  61.1 8.8 %all_to_all.35 = f32[32,1,128]{2,1,0:T(1,128)S(1)} all-to-all(f32[32,1,128]{2,1,0:T(1,128)S(1)} %bitcast.35), channel_id=1, replica_groups=mesh['ray'=4,'vox'=8] {'ray','vox'}, dimensions={0} | all-to-all | bytes 32768 | tf_op jit(solution)/shard_map/all_to_all | solution.py:349
  69.9 0.0 collective-permute-done.2.refs_3_
  69.9 0.0 collective-permute-done.1.refs_2_
  69.9 0.0 collective-permute-done.refs_1_
  69.9 0.7 %final.1 = (f32[64,128]{1,0:T(8,128)}, f32[64,128]{1,0:T(8,128)}) custom-call(f32[32,128]{1,0:T(8,128)S(1)} %bitcast.34, f32[192,128]{1,0:T(8,128)S(1)} %get-tuple-element.35.refs_0_, f32[192,128]{1,0:T(8,128)S(1)} %collective-permute-done.refs_1_, f32[192,128]{1,0:T(8,128)S(1)} %collective-permute-done.1.refs_2_, f32[192,128]{1,0:T(8,128)S(1)} %collective-permute-done.2.refs_3_), custom_call_target="tpu_custom_call" | custom-call | tf_op jit(solution)/shard_map/final/pallas_call | solution.py:342
Async XLA Ops:
  59.1 10.8 %collective-permute-start.2 = (f32[192,128]{1,0:T(8,128)S(1)}, f32[192,128]{1,0:T(8,128)S(1)}, u32[]{:S(2)}, u32[]{:S(2)}) collective-permute-start(f32[192,128]{1,0:T(8,128)S(1)} %get-tuple-element.35.refs_0_), channel_id=1, source_target_pairs={{0,24},{8,16},{16,8},{24,0},{1,25},{9,17},{17,9},{25,1},{2,26},{10... | collective-permute-start | bytes 294920 | tf_op jit(solution)/shard_map/ppermute | solution.py:395
  59.5 10.4 %collective-permute-start.1 = (f32[192,128]{1,0:T(8,128)S(1)}, f32[192,128]{1,0:T(8,128)S(1)}, u32[]{:S(2)}, u32[]{:S(2)}) collective-permute-start(f32[192,128]{1,0:T(8,128)S(1)} %get-tuple-element.35.refs_0_), channel_id=1, source_target_pairs={{0,16},{8,24},{16,0},{24,8},{1,17},{9,25},{17,1},{25,9},{2,18},{10... | collective-permute-start | bytes 294920 | tf_op jit(solution)/shard_map/ppermute | solution.py:395
  60.9 9.0 %collective-permute-start = (f32[192,128]{1,0:T(8,128)S(1)}, f32[192,128]{1,0:T(8,128)S(1)}, u32[]{:S(2)}, u32[]{:S(2)}) collective-permute-start(f32[192,128]{1,0:T(8,128)S(1)} %get-tuple-element.35.refs_0_), channel_id=1, source_target_pairs={{0,8},{8,0},{16,24},{24,16},{1,9},{9,1},{17,25},{25,17},{2,10},{10... | collective-permute-start | bytes 294920 | tf_op jit(solution)/shard_map/ppermute | solution.py:395

commit v8 on v5

--- a/solution.py
+++ b/solution.py
@@ -123,6 +123,7 @@
     by_col = pad[...].T
     for r in range(z.ray_blocks):
         wide[r] = jnp.broadcast_to(by_col[:, r : r + 1], (LANES, LANES))
+    square = total(travel[...] * travel[...])
     for copy in small[1:]:
         copy.wait()
 
@@ -143,7 +144,7 @@
     code[pl.ds(z.slots, 1), :] = jnp.full((1, LANES), groups, jnp.int32)
     backward(groups, where_of, tiles_v, wide, prod, ready)
     here = lane((z.n_vox, LANES))
-    meta = jnp.where(here == z.cap, total(travel[...] * travel[...]), 0.0)
+    meta = jnp.where(here == z.cap, square, 0.0)
     for k in range(z.cap):
         meta = jnp.where(here == k, named[pl.ds(k * z.n_vox, z.n_vox), :], meta)
     write_products(z, prod, msg, meta)

time: 70.3 us -> 70.1 us (level)
  Pallas kernels: 7.52 us -> 6.18 us
    pallas_call x7, Pallas kernels: 7.52 us -> 6.18 us  [call(): pl.pallas_call(functools.partial(kernel, z), name=name, in_specs=in_specs...]
    all_to_all x6, blocking collectives: 59.5 us -> 60.2 us  [exchange(): lax.all_to_all(x.reshape(n, 1, LANES), ('ray', 'vox'), 0, 0, tiled=True)]
where the time goes in v8:
time: 70.1 us; the launch traced here: 69.7 us
  blocking collectives  60.2 us (86%)
  Pallas kernels  6.18 us (9%)
  starting transfers between devices  1.96 us (3%)
  between operations  1.32 us (2%)
    all_to_all x6, blocking collectives, exchange(): lax.all_to_all(x.reshape(n, 1, LANES), ('ray', 'vox'), 0, 0, tiled=True)  60.2 us
    pallas_call x7, Pallas kernels, call(): pl.pallas_call(functools.partial(kernel, z), name=name, in_specs=in_specs...  6.18 us
    ppermute x3, starting transfers between devices, on_device(): lax.ppermute(share, 'ray', [(r, r ^ hop) for r in range(n_ray)])  1.96 us
  transfers between devices with their start and end apart: 3, of which 0 were waited for; matrix products, arithmetic and copies ran while one was open for 0% of the time, Pallas kernels for 0%

profile of v8, /device:TPU:0, one launch (start us, length us, event | category | flops | bytes accessed | tf_op | source)
XLA Modules:
  0.0 69.7 jit_solution(14124496214689163903)
XLA Ops:
  1.3 1.9 %first.1 = (f32[160,128]{1,0:T(8,128)S(1)}, f32[16,128,128]{2,1,0:T(8,128)S(1)}, s32[72,128]{1,0:T(8,128)S(1)}, f32[64,128,128]{2,1,0:T(8,128)S(1)}) custom-call(s32[64]{0:T(128)} %ray_hbm.1, s32[64]{0:T(128)} %vox_hbm.1, s32[1]{0:T(128)S(6)} %copy.13.tile_count, f32[16,128]{1,0:T(8,128)} %travel_hbm.1, f32[64,128,128]{2,1,0:T(8,128)} %tiles_hbm.1), custom_call_target="tpu_custom_call" | custom-call | tf_op jit(solution)/shard_map/first/pallas_call | solution.py:339
  3.2 14.5 %all_to_all.30 = f32[160,1,128]{2,1,0:T(1,128)S(1)} all-to-all(f32[160,1,128]{2,1,0:T(1,128)S(1)} %bitcast.30), channel_id=1, replica_groups=mesh['ray'=4,'vox'=8] {'ray','vox'}, dimensions={0} | all-to-all | bytes 163840 | tf_op jit(solution)/shard_map/all_to_all | solution.py:346
  17.7 0.7 %owner1.1 = (f32[160,128]{1,0:T(8,128)S(1)}, f32[64,128]{1,0:T(8,128)S(1)}, bf16[256,128]{1,0:T(8,128)(2,1)S(1)}, bf16[128,256]{1,0:T(8,128)(2,1)S(1)}) custom-call(f32[160,128]{1,0:T(8,128)S(1)} %bitcast.25), custom_call_target="tpu_custom_call" | custom-call | tf_op jit(solution)/shard_map/owner1/pallas_call | solution.py:339
  18.4 9.1 %all_to_all.31 = f32[160,1,128]{2,1,0:T(1,128)S(1)} all-to-all(f32[160,1,128]{2,1,0:T(1,128)S(1)} %bitcast.31), channel_id=1, replica_groups=mesh['ray'=4,'vox'=8] {'ray','vox'}, dimensions={0} | all-to-all | bytes 163840 | tf_op jit(solution)/shard_map/all_to_all | solution.py:346
  27.6 0.9 %middle1.1 = (f32[160,128]{1,0:T(8,128)S(1)}, f32[8,128]{1,0:T(8,128)S(1)}, f32[16,128,128]{2,1,0:T(8,128)S(1)}) custom-call(s32[72,128]{1,0:T(8,128)S(1)} %get-tuple-element.19.code_v, f32[160,128]{1,0:T(8,128)S(1)} %bitcast.28, f32[16,128,128]{2,1,0:T(8,128)S(1)} %get-tuple-element.22.old, f32[64,128,128]{2,1,0:T(8,128)S(1)} %get-tuple-element.23.tiles_v), custom_call_target="tpu_custom_call" | custom-call | tf_op jit(solution)/shard_map/middle1/pallas_call | solution.py:339
  28.5 9.3 %all_to_all.32 = f32[160,1,128]{2,1,0:T(1,128)S(1)} all-to-all(f32[160,1,128]{2,1,0:T(1,128)S(1)} %bitcast.32), channel_id=1, replica_groups=mesh['ray'=4,'vox'=8] {'ray','vox'}, dimensions={0} | all-to-all | bytes 163840 | tf_op jit(solution)/shard_map/all_to_all | solution.py:346
  37.8 0.5 owner2.1
  38.3 9.1 %all_to_all.33 = f32[160,1,128]{2,1,0:T(1,128)S(1)} all-to-all(f32[160,1,128]{2,1,0:T(1,128)S(1)} %bitcast.33), channel_id=1, replica_groups=mesh['ray'=4,'vox'=8] {'ray','vox'}, dimensions={0} | all-to-all | bytes 163840 | tf_op jit(solution)/shard_map/all_to_all | solution.py:346
  47.5 1.0 %middle2.1 = (f32[160,128]{1,0:T(8,128)S(1)}, f32[8,128]{1,0:T(8,128)S(1)}) custom-call(s32[72,128]{1,0:T(8,128)S(1)} %get-tuple-element.19.code_v, f32[160,128]{1,0:T(8,128)S(1)} %bitcast.27, f32[16,128,128]{2,1,0:T(8,128)S(1)} %get-tuple-element.30.old, f32[64,128,128]{2,1,0:T(8,128)S(1)} %get-tuple-element.23.tiles_v), custom_call_target="tpu_custom_call" | custom-call | tf_op jit(solution)/shard_map/middle2/pallas_call | solution.py:339
  48.4 9.4 %all_to_all.34 = f32[160,1,128]{2,1,0:T(1,128)S(1)} all-to-all(f32[160,1,128]{2,1,0:T(1,128)S(1)} %bitcast.29), channel_id=1, replica_groups=mesh['ray'=4,'vox'=8] {'ray','vox'}, dimensions={0} | all-to-all | bytes 163840 | tf_op jit(solution)/shard_map/all_to_all | solution.py:346
  57.8 0.4 owner3.1
  58.2 0.3 collective-permute-start.2
  58.5 1.5 %collective-permute-start.1 = (f32[192,128]{1,0:T(8,128)S(1)}, f32[192,128]{1,0:T(8,128)S(1)}, u32[]{:S(2)}, u32[]{:S(2)}) collective-permute-start(f32[192,128]{1,0:T(8,128)S(1)} %get-tuple-element.35.refs_0_), channel_id=1, source_target_pairs={{0,16},{8,24},{16,0},{24,8},{1,17},{9,25},{17,1},{25,9},{2,18},{10... | collective-permute-start | bytes 294920 | tf_op jit(solution)/shard_map/ppermute | solution.py:392
  60.0 0.1 collective-permute-start
  60.2 8.8 %all_to_all.35 = f32[32,1,128]{2,1,0:T(1,128)S(1)} all-to-all(f32[32,1,128]{2,1,0:T(1,128)S(1)} %bitcast.35), channel_id=1, replica_groups=mesh['ray'=4,'vox'=8] {'ray','vox'}, dimensions={0} | all-to-all | bytes 32768 | tf_op jit(solution)/shard_map/all_to_all | solution.py:346
  69.0 0.0 collective-permute-done.2.refs_3_
  69.0 0.0 collective-permute-done.1.refs_2_
  69.0 0.0 collective-permute-done.refs_1_
  69.0 0.7 %final.1 = (f32[64,128]{1,0:T(8,128)}, f32[64,128]{1,0:T(8,128)}) custom-call(f32[32,128]{1,0:T(8,128)S(1)} %bitcast.34, f32[192,128]{1,0:T(8,128)S(1)} %get-tuple-element.35.refs_0_, f32[192,128]{1,0:T(8,128)S(1)} %collective-permute-done.refs_1_, f32[192,128]{1,0:T(8,128)S(1)} %collective-permute-done.1.refs_2_, f32[192,128]{1,0:T(8,128)S(1)} %collective-permute-done.2.refs_3_), custom_call_target="tpu_custom_call" | custom-call | tf_op jit(solution)/shard_map/final/pallas_call | solution.py:339
Async XLA Ops:
  58.2 10.8 %collective-permute-start.2 = (f32[192,128]{1,0:T(8,128)S(1)}, f32[192,128]{1,0:T(8,128)S(1)}, u32[]{:S(2)}, u32[]{:S(2)}) collective-permute-start(f32[192,128]{1,0:T(8,128)S(1)} %get-tuple-element.35.refs_0_), channel_id=1, source_target_pairs={{0,24},{8,16},{16,8},{24,0},{1,25},{9,17},{17,9},{25,1},{2,26},{10... | collective-permute-start | bytes 294920 | tf_op jit(solution)/shard_map/ppermute | solution.py:392
  58.5 10.4 %collective-permute-start.1 = (f32[192,128]{1,0:T(8,128)S(1)}, f32[192,128]{1,0:T(8,128)S(1)}, u32[]{:S(2)}, u32[]{:S(2)}) collective-permute-start(f32[192,128]{1,0:T(8,128)S(1)} %get-tuple-element.35.refs_0_), channel_id=1, source_target_pairs={{0,16},{8,24},{16,0},{24,8},{1,17},{9,25},{17,1},{25,9},{2,18},{10... | collective-permute-start | bytes 294920 | tf_op jit(solution)/shard_map/ppermute | solution.py:392
  60.0 9.0 %collective-permute-start = (f32[192,128]{1,0:T(8,128)S(1)}, f32[192,128]{1,0:T(8,128)S(1)}, u32[]{:S(2)}, u32[]{:S(2)}) collective-permute-start(f32[192,128]{1,0:T(8,128)S(1)} %get-tuple-element.35.refs_0_), channel_id=1, source_target_pairs={{0,8},{8,0},{16,24},{24,16},{1,9},{9,1},{17,25},{25,17},{2,10},{10... | collective-permute-start | bytes 294920 | tf_op jit(solution)/shard_map/ppermute | solution.py:392
